TPU v7x, 32 devices: a whole 2x2x4 slice. The times are simulated.
32 devices in a mesh: regroup: 2 (over y), loop: 4 (over z), replica: 4 (over x, core).
Axes of the slice: x: 2, y: 2, z: 4, core: 2. Of those that a mesh axis runs over, the one named last changes fastest.
Arguments:
- features: bfloat16 [4, 4, 1024, 256], P('replica', 'loop', None, 'regroup'), may hold values from -6 to 6
- weight: bfloat16 [256, 256], replicated, may hold values from -0.375 to 0.375
- tiles: bfloat16 [4, 4, 2, 32, 128, 128], P('replica', 'loop', 'regroup'), may hold values from 0 to 1, as said below
- tile_row: int32 [4, 4, 2, 32], P('replica', 'loop', 'regroup'), may hold values from 0 to 3, as said below
- tile_col: int32 [4, 4, 2, 32], P('replica', 'loop', 'regroup'), may hold values from 0 to 3, as said below
- tile_width: int32 [4, 4, 2, 32], P('replica', 'loop', 'regroup'), may hold values from 0 to 128, as said below
- cotangent: bfloat16 [4, 4, 2, 512, 256], P('replica', 'loop', 'regroup'), may hold values from -6 to 6
Outputs:
- output: bfloat16 [4, 4, 2, 512, 256], P('replica', 'loop', 'regroup')
- grad_feat: bfloat16 [4, 4, 1024, 256], P('replica', 'loop', None, 'regroup')
- grad_weight: float32 [256, 256], replicated
Inputs may be any that keep to these rules, and one draw needn't show every extreme that they name: `tiles`: entries are 0 or between 0.25 and 1. `tile_row`: slot k < 4 of every device names cell block k. tile_col[r, l, g, s] is l - 1, l or l + 1 modulo 4. `tile_width`: each device's live slots come first, from 4 to 32 of them; some device has exactly 4 live and some all 32; slot 0 is live with width 128.
All inputs are finite; a program needn't handle non-finite values.
Results may differ from a plain program's by a relative error of at most 0.013.
Values may be sent and summed in bfloat16 or wider, within the bound.
A program may use at most 64 MiB of HBM per device.

v0:
```python
import math

import jax
import jax.numpy as jnp
from jax import lax
from jax.sharding import PartitionSpec as P

EPSILON = 1e-06


def shifted(block, axis, distance):
    devices = range(lax.axis_size(axis))
    route = [((i - distance) % len(devices), i) for i in devices]
    return lax.ppermute(block, axis, route)


def rms_scale(values):
    return values * lax.rsqrt(jnp.mean(values * values, axis=-1, keepdims=True) + EPSILON)


def per_device(features, weight, tiles, tile_row, tile_col, tile_width, cotangent):
    cell_rows = lax.all_to_all(features, "regroup", split_axis=2, concat_axis=3, tiled=True)[0, 0]
    cells, width = cell_rows.shape
    edge = tiles.shape[-1]
    blocks = cells // edge
    loops = lax.axis_size("loop")
    high = lax.Precision.HIGHEST
    rows_idx = tile_row[0, 0, 0]
    cols_idx = tile_col[0, 0, 0]
    widths = tile_width[0, 0, 0]
    column = jnp.arange(edge, dtype=jnp.int32)
    live_tiles = jnp.where(
        column[None, None, :] < widths[:, None, None], tiles[0, 0, 0], jnp.zeros((), tiles.dtype)
    )
    row_hot = (rows_idx[:, None] == jnp.arange(blocks, dtype=jnp.int32)[None, :]).astype(
        jnp.float32
    )
    row_sums = jnp.sum(live_tiles, axis=2, dtype=jnp.float32)
    cell_deg = 1.0 + jnp.einsum("tr,ti->ri", row_hot, row_sums, precision=high).reshape(cells)
    cell_root = jnp.sqrt(cell_deg)[:, None]
    col_tile_sums = jnp.sum(live_tiles, axis=1, dtype=jnp.float32)

    def to_nets(values, hot):
        gathered = values.reshape(blocks, edge, width)[rows_idx]
        per_tile = jnp.einsum(
            "tij,tif->tjf", live_tiles, gathered, preferred_element_type=jnp.float32
        )
        return jnp.einsum("tc,tjf->cjf", hot, per_tile, precision=high)

    def from_nets(blocked, index):
        gathered = blocked[index]
        per_tile = jnp.einsum(
            "tij,tjf->tif", live_tiles, gathered, preferred_element_type=jnp.float32
        )
        return jnp.einsum("tr,tif->rif", row_hot, per_tile, precision=high).reshape(cells, width)

    mixed = jnp.dot(cell_rows, weight, preferred_element_type=jnp.float32).astype(jnp.bfloat16)
    scaled = (mixed.astype(jnp.float32) / cell_root).astype(jnp.bfloat16)
    place = (cols_idx - lax.axis_index("loop") + loops) % loops
    net_index = jnp.where(place == 0, 1, jnp.where(place == 1, 2, 0)).astype(jnp.int32)
    near_hot = (net_index[:, None] == jnp.arange(3, dtype=jnp.int32)[None, :]).astype(jnp.float32)
    near_terms = to_nets(scaled, near_hot).astype(jnp.bfloat16)
    near_degs = jnp.einsum("tc,tj->cj", near_hot, col_tile_sums, precision=high).astype(
        jnp.bfloat16
    )
    below = shifted((near_terms[2], near_degs[2]), "loop", 1)
    above = shifted((near_terms[0], near_degs[0]), "loop", -1)
    totals = (
        near_terms[1].astype(jnp.float32)
        + below[0].astype(jnp.float32)
        + above[0].astype(jnp.float32)
    )
    degrees = (
        near_degs[1].astype(jnp.float32)
        + below[1].astype(jnp.float32)
        + above[1].astype(jnp.float32)
    )
    net_deg = (1.0 + degrees)[:, None]
    own_feat = (totals / net_deg).astype(jnp.bfloat16)
    prev_feat = shifted(own_feat, "loop", 1)
    next_feat = shifted(own_feat, "loop", -1)
    net_feat = jnp.stack([prev_feat, own_feat, next_feat])
    gathered_z = from_nets(net_feat, net_index) / cell_root
    normed, norm_back = jax.vjp(rms_scale, gathered_z)
    before = mixed.astype(jnp.float32) + normed
    output = jax.nn.silu(before).astype(jnp.bfloat16)
    sigmoid_v = jax.nn.sigmoid(before)
    grad_before = (
        cotangent[0, 0, 0].astype(jnp.float32) * sigmoid_v * (1.0 + before * (1.0 - sigmoid_v))
    )
    grad_z = norm_back(grad_before)[0]
    grad_scaled = (grad_z / cell_root).astype(jnp.bfloat16)
    grad_near = to_nets(grad_scaled, near_hot).astype(jnp.bfloat16)
    grad_below = shifted(grad_near[2], "loop", 1)
    grad_above = shifted(grad_near[0], "loop", -1)
    grad_sum_own = (
        grad_near[1].astype(jnp.float32)
        + grad_below.astype(jnp.float32)
        + grad_above.astype(jnp.float32)
    )
    grad_own = (grad_sum_own / net_deg).astype(jnp.bfloat16)
    grad_prev = shifted(grad_own, "loop", 1)
    grad_next = shifted(grad_own, "loop", -1)
    grad_net = jnp.stack([grad_prev, grad_own, grad_next])
    grad_mixed = (grad_before + from_nets(grad_net, net_index) / cell_root).astype(jnp.bfloat16)
    grad_rows = jnp.einsum(
        "cg,fg->cf", grad_mixed, weight, preferred_element_type=jnp.float32
    ).astype(jnp.bfloat16)
    grad_feat = lax.all_to_all(
        grad_rows[None, None], "regroup", split_axis=3, concat_axis=2, tiled=True
    )
    weight_term = jnp.einsum("cf,cg->fg", cell_rows, grad_mixed, preferred_element_type=jnp.float32)
    weight_part = lax.psum_scatter(
        weight_term, ("regroup", "loop"), scatter_dimension=0, tiled=True
    )
    weight_part = lax.psum(weight_part, "replica")
    weight_sum = lax.all_gather(weight_part, ("regroup", "loop"), axis=0, tiled=True)
    total_cells = cells * lax.axis_size("regroup") * loops * lax.axis_size("replica")
    grad_weight = weight_sum * (1.0 / math.sqrt(total_cells))
    return (output[None, None, None], grad_feat, grad_weight)


def solution(mesh):
    return jax.shard_map(
        per_device,
        mesh=mesh,
        in_specs=(
            P("replica", "loop", None, "regroup"),
            P(),
            P("replica", "loop", "regroup", None, None, None),
            P("replica", "loop", "regroup", None),
            P("replica", "loop", "regroup", None),
            P("replica", "loop", "regroup", None),
            P("replica", "loop", "regroup", None, None),
        ),
        out_specs=(
            P("replica", "loop", "regroup", None, None),
            P("replica", "loop", None, "regroup"),
            P(),
        ),
        check_vma=False,
    )
```

profile of v0, /device:TPU:0, one launch (start us, length us, event | category | flops | bytes accessed | tf_op | source)
XLA Modules:
  0.0 198.6 jit_solution(6420533877653232573)
XLA Ops:
  11.0 3.0 %collective-permute-start.2 = (bf16[128]{0:T(256)(128)(2,1)}, bf16[128]{0:T(256)(128)(2,1)}, u32[]{:S(2)}, u32[]{:S(2)}) collective-permute-start(bf16[128]{0:T(256)(128)(2,1)} %get-tuple-element.22), channel_id=1, source_target_pairs={{12,0},{0,4},{4,8},{8,12},{13,1},{1,5},{5,9},{9,13},{14,2},{2,6},{... | collective-permute-start | bytes 776 | tf_op jit(solution)/shard_map/ppermute | solution.py:14
  14.0 2.0 %collective-permute-start.3 = (bf16[128]{0:T(256)(128)(2,1)}, bf16[128]{0:T(256)(128)(2,1)}, u32[]{:S(2)}, u32[]{:S(2)}) collective-permute-start(bf16[128]{0:T(256)(128)(2,1)} %get-tuple-element.23), channel_id=1, source_target_pairs={{4,0},{8,4},{12,8},{0,12},{5,1},{9,5},{13,9},{1,13},{6,2},{10,6},{... | collective-permute-start | bytes 776 | tf_op jit(solution)/shard_map/ppermute | solution.py:14
  17.9 2.3 %reduce.1 = bf16[1024,128]{1,0:T(8,128)(2,1)S(1)} reduce(bf16[1024,1,1,128]{3,2,1,0:T(2,128)(2,1)S(1)} %bitcast.136, bf16[]{:T(256)} %broadcast.232), dimensions={1,2}, to_apply=%bitcast.131.reduce_sub_computation | reduce | bytes 524290
  20.9 3.4 %all-to-all-start = ((bf16[2,2,32768]{2,1,0:T(2,128)(2,1)}), bf16[2,2,32768]{2,1,0:T(2,128)(2,1)S(1)}, u32[]{:S(2)}, u32[]{:S(2)}) async-start(bf16[2,2,32768]{2,1,0:T(2,128)(2,1)} %reshape.232), calls=%async_computation | async-start | bytes 524288 | tf_op jit(solution)/shard_map/all_to_all | solution.py:22
  25.9 3.6 %all-to-all-done = bf16[2,2,32768]{2,1,0:T(2,128)(2,1)S(1)} async-done(((bf16[2,2,32768]{2,1,0:T(2,128)(2,1)}), bf16[2,2,32768]{2,1,0:T(2,128)(2,1)S(1)}, u32[]{:S(2)}, u32[]{:S(2)}) %all-to-all-start) | async-done | bytes 262176 | tf_op jit(solution)/shard_map/all_to_all | solution.py:22
  33.1 3.8 %fusion.9 = bf16[3,128,256]{2,0,1:T(4,128)(2,1)S(1)} fusion(f32[32,128,256]{2,1,0:T(8,128)S(1)} %fusion.23, s32[32]{0:T(128)S(1)} %copy-done.10), kind=kOutput, calls=%fused_computation.17 | convolution fusion | flops 37847136 | bytes 4391040 | tf_op jit(solution)/shard_map/tc,tjf->cjf/dot_general | solution.py:48
  37.3 2.1 %collective-permute-start.1 = (bf16[128,256]{1,0:T(8,128)(2,1)S(1)}, bf16[128,256]{1,0:T(8,128)(2,1)S(1)}, u32[]{:S(2)}, u32[]{:S(2)}) collective-permute-start(bf16[128,256]{1,0:T(8,128)(2,1)S(1)} %bitcast.146), channel_id=1, source_target_pairs={{4,0},{8,4},{12,8},{0,12},{5,1},{9,5},{13,9},{1,13},{6,2},{10,6},{... | collective-permute-start | bytes 196616 | tf_op jit(solution)/shard_map/ppermute | solution.py:14
  41.6 3.8 %collective-permute-done = bf16[128,256]{1,0:T(8,128)(2,1)S(1)} collective-permute-done((bf16[128,256]{1,0:T(8,128)(2,1)S(1)}, bf16[128,256]{1,0:T(8,128)(2,1)S(1)}, u32[]{:S(2)}, u32[]{:S(2)}) %collective-permute-start) | collective-permute-done | bytes 65568 | tf_op jit(solution)/shard_map/ppermute | solution.py:14
  45.6 2.0 %collective-permute-start.4 = (bf16[128,256]{1,0:T(8,128)(2,1)S(1)}, bf16[128,256]{1,0:T(8,128)(2,1)S(1)}, u32[]{:S(2)}, u32[]{:S(2)}) collective-permute-start(bf16[128,256]{1,0:T(8,128)(2,1)S(1)} %fusion.27), channel_id=1, source_target_pairs={{12,0},{0,4},{4,8},{8,12},{13,1},{1,5},{5,9},{9,13},{14,2},{2,6},{... | collective-permute-start | bytes 196616 | tf_op jit(solution)/shard_map/ppermute | solution.py:14
  47.6 2.2 %collective-permute-done.5 = bf16[128,256]{1,0:T(8,128)(2,1)S(1)} collective-permute-done((bf16[128,256]{1,0:T(8,128)(2,1)S(1)}, bf16[128,256]{1,0:T(8,128)(2,1)S(1)}, u32[]{:S(2)}, u32[]{:S(2)}) %collective-permute-start.5) | collective-permute-done | bytes 65568 | tf_op jit(solution)/shard_map/ppermute | solution.py:14
  49.8 2.0 %collective-permute-done.4 = bf16[128,256]{1,0:T(8,128)(2,1)S(1)} collective-permute-done((bf16[128,256]{1,0:T(8,128)(2,1)S(1)}, bf16[128,256]{1,0:T(8,128)(2,1)S(1)}, u32[]{:S(2)}, u32[]{:S(2)}) %collective-permute-start.4) | collective-permute-done | bytes 65568 | tf_op jit(solution)/shard_map/ppermute | solution.py:14
  53.5 4.0 %fusion.19 = (f32[4,128]{0,1:T(8,128)S(1)}, f32[4,128,256]{2,0,1:T(4,128)S(1)}) fusion(f32[4,128]{0,1:T(8,128)S(1)} %copy-done.8, f32[32,128,256]{2,1,0:T(8,128)S(1)} %fusion.22, s32[32]{0:T(128)S(1)} %bitcast.156), kind=kOutput, calls=%fused_computation.39 | convolution fusion | flops 50724480 | bytes 4722816 | tf_op jit(solution)/shard_map/tr,tif->rif/dot_general | solution.py:55
  61.1 3.8 %fusion.2 = bf16[3,128,256]{2,0,1:T(4,128)(2,1)S(1)} fusion(f32[32,128,256]{2,1,0:T(8,128)S(1)} %fusion.21, s32[32]{0:T(128)S(1)} %copy-done.11), kind=kOutput, calls=%fused_computation.6 | convolution fusion | flops 37748832 | bytes 4391040 | tf_op jit(solution)/shard_map/tc,tjf->cjf/dot_general | solution.py:48
  65.0 3.8 %collective-permute-start.7 = (bf16[128,256]{1,0:T(8,128)(2,1)S(1)}, bf16[128,256]{1,0:T(8,128)(2,1)S(1)}, u32[]{:S(2)}, u32[]{:S(2)}) collective-permute-start(bf16[128,256]{1,0:T(8,128)(2,1)S(1)} %get-tuple-element.21), channel_id=1, source_target_pairs={{4,0},{8,4},{12,8},{0,12},{5,1},{9,5},{13,9},{1,13},{6,2},{10,6},{... | collective-permute-start | bytes 196616 | tf_op jit(solution)/shard_map/ppermute | solution.py:14
  68.9 2.2 %collective-permute-done.6 = bf16[128,256]{1,0:T(8,128)(2,1)S(1)} collective-permute-done((bf16[128,256]{1,0:T(8,128)(2,1)S(1)}, bf16[128,256]{1,0:T(8,128)(2,1)S(1)}, u32[]{:S(2)}, u32[]{:S(2)}) %collective-permute-start.6) | collective-permute-done | bytes 65568 | tf_op jit(solution)/shard_map/ppermute | solution.py:14
  71.2 4.2 %collective-permute-start.9 = (bf16[128,256]{1,0:T(8,128)(2,1)S(1)}, bf16[128,256]{1,0:T(8,128)(2,1)S(1)}, u32[]{:S(2)}, u32[]{:S(2)}) collective-permute-start(bf16[128,256]{1,0:T(8,128)(2,1)S(1)} %fusion.30), channel_id=1, source_target_pairs={{4,0},{8,4},{12,8},{0,12},{5,1},{9,5},{13,9},{1,13},{6,2},{10,6},{... | collective-permute-start | bytes 196616 | tf_op jit(solution)/shard_map/ppermute | solution.py:14
  75.4 1.9 collective-permute-done.9
  77.3 4.2 %collective-permute-done.8 = bf16[128,256]{1,0:T(8,128)(2,1)S(1)} collective-permute-done((bf16[128,256]{1,0:T(8,128)(2,1)S(1)}, bf16[128,256]{1,0:T(8,128)(2,1)S(1)}, u32[]{:S(2)}, u32[]{:S(2)}) %collective-permute-start.8) | collective-permute-done | bytes 65568 | tf_op jit(solution)/shard_map/ppermute | solution.py:14
  82.9 3.8 %fusion = f32[4,128,256]{2,0,1:T(4,128)S(1)} fusion(f32[32,128,256]{2,1,0:T(8,128)S(1)} %fusion.20, s32[32]{0:T(128)S(1)} %bitcast.157), kind=kOutput, calls=%fused_computation.4 | convolution fusion | flops 50331776 | bytes 4718720 | tf_op jit(solution)/shard_map/tr,tif->rif/dot_general | solution.py:55
  89.5 2.2 %reduce.2 = bf16[256,512]{1,0:T(8,128)(2,1)S(1)} reduce(bf16[256,1,1,512]{3,2,1,0:T(2,128)(2,1)S(1)} %bitcast.137, bf16[]{:T(256)} %broadcast.232), dimensions={1,2}, to_apply=%bitcast.110.reduce_sub_computation | reduce | bytes 524290
  91.9 7.6 %all_to_all.33 = bf16[2,2,32768]{2,1,0:T(2,128)(2,1)S(1)} all-to-all(bf16[2,2,32768]{2,1,0:T(2,128)(2,1)S(1)} %reshape.234), channel_id=1, replica_groups=mesh['regroup'=2,'loop'=4,'replica'=4] {'regroup'}, dimensions={0} | all-to-all | bytes 524288 | tf_op jit(solution)/shard_map/all_to_all | solution.py:109
  100.6 46.8 %reduce-scatter.4.cloned.1.call-done = f32[32,256]{1,0:T(8,128)} async-done(((f32[256,256]{1,0:T(8,128)}), f32[32,256]{1,0:T(8,128)}) %reduce-scatter.4.cloned.1.call-update) | async-done | bytes 32784
  148.2 11.5 %psum.7 = f32[32,256]{0,1:T(8,128)S(1)} all-reduce(f32[32,256]{0,1:T(8,128)S(1)} %copy.103), channel_id=1, replica_groups=mesh['regroup'=2,'loop'=4,'replica'=4] {'replica'}, use_global_device_ids=true, to_apply=%region_5.6 | all-reduce | flops 8192 | bytes 65536 | tf_op jit(solution)/shard_map/psum | solution.py:116
  159.8 31.3 %all_gather.3 = f32[256,256]{1,0:T(8,128)S(1)} all-gather(f32[32,256]{1,0:T(8,128)S(1)} %copy.99), channel_id=1, replica_groups=mesh['regroup'=2,'loop'=4,'replica'=4] {'regroup','loop'}, dimensions={0}, use_global_device_ids=true | all-gather | bytes 294912 | tf_op jit(solution)/shard_map/all_gather | solution.py:117
  (104 shorter events, 26.5 us)
Async XLA Ops:
  7.2 22.9 %copy-start = (bf16[256,256]{1,0:T(8,128)(2,1)S(1)}, bf16[256,256]{1,0:T(8,128)(2,1)}, u32[]{:S(2)}) copy-start(bf16[256,256]{1,0:T(8,128)(2,1)} %param.8) | copy-start | bytes 393220
  7.2 17.3 %copy-start.18 = (s32[1,1,1,32]{3,2,1,0:T(1,128)S(1)}, s32[1,1,1,32]{3,2,1,0:T(1,128)}, u32[]{:S(2)}) copy-start(s32[1,1,1,32]{3,2,1,0:T(1,128)} %param.11) | copy-start | bytes 388
  7.2 17.8 %copy-start.14 = (s32[1,1,1,32]{3,2,1,0:T(1,128)S(1)}, s32[1,1,1,32]{3,2,1,0:T(1,128)}, u32[]{:S(2)}) copy-start(s32[1,1,1,32]{3,2,1,0:T(1,128)} %param.10) | copy-start | bytes 388
  8.6 16.4 %copy-start.9 = (s32[32]{0:T(128)}, s32[32]{0:T(128)S(1)}, u32[]{:S(2)}) copy-start(s32[32]{0:T(128)S(1)} %compare_select_fusion.8) | copy-start | bytes 388
  11.0 28.4 %collective-permute-start.2 = (bf16[128]{0:T(256)(128)(2,1)}, bf16[128]{0:T(256)(128)(2,1)}, u32[]{:S(2)}, u32[]{:S(2)}) collective-permute-start(bf16[128]{0:T(256)(128)(2,1)} %get-tuple-element.22), channel_id=1, source_target_pairs={{12,0},{0,4},{4,8},{8,12},{13,1},{1,5},{5,9},{9,13},{14,2},{2,6},{... | collective-permute-start | bytes 776 | tf_op jit(solution)/shard_map/ppermute | solution.py:14
  14.0 25.4 %collective-permute-start.3 = (bf16[128]{0:T(256)(128)(2,1)}, bf16[128]{0:T(256)(128)(2,1)}, u32[]{:S(2)}, u32[]{:S(2)}) collective-permute-start(bf16[128]{0:T(256)(128)(2,1)} %get-tuple-element.23), channel_id=1, source_target_pairs={{4,0},{8,4},{12,8},{0,12},{5,1},{9,5},{13,9},{1,13},{6,2},{10,6},{... | collective-permute-start | bytes 776 | tf_op jit(solution)/shard_map/ppermute | solution.py:14
  20.9 8.6 %all-to-all-start = ((bf16[2,2,32768]{2,1,0:T(2,128)(2,1)}), bf16[2,2,32768]{2,1,0:T(2,128)(2,1)S(1)}, u32[]{:S(2)}, u32[]{:S(2)}) async-start(bf16[2,2,32768]{2,1,0:T(2,128)(2,1)} %reshape.232), calls=%async_computation | async-start | bytes 524288 | tf_op jit(solution)/shard_map/all_to_all | solution.py:22
  24.4 123.0 %reduce-scatter.4.cloned.1.call-start = ((), (), s32[]{:S(2)}) async-start(), calls=%async_computation.3 | async-start | bytes 294912
  30.0 1.1 copy-start.4
  31.1 1.2 copy-start.1
  33.1 14.5 %copy-start.17 = (s32[32]{0:T(128)S(1)}, s32[32]{0:T(128)}, u32[]{:S(2)}) copy-start(s32[32]{0:T(128)} %fusion.43) | copy-start | bytes 388
  37.3 4.3 %collective-permute-start.1 = (bf16[128,256]{1,0:T(8,128)(2,1)S(1)}, bf16[128,256]{1,0:T(8,128)(2,1)S(1)}, u32[]{:S(2)}, u32[]{:S(2)}) collective-permute-start(bf16[128,256]{1,0:T(8,128)(2,1)S(1)} %bitcast.146), channel_id=1, source_target_pairs={{4,0},{8,4},{12,8},{0,12},{5,1},{9,5},{13,9},{1,13},{6,2},{10,6},{... | collective-permute-start | bytes 196616 | tf_op jit(solution)/shard_map/ppermute | solution.py:14
  39.4 6.1 %collective-permute-start = (bf16[128,256]{1,0:T(8,128)(2,1)S(1)}, bf16[128,256]{1,0:T(8,128)(2,1)S(1)}, u32[]{:S(2)}, u32[]{:S(2)}) collective-permute-start(bf16[128,256]{1,0:T(8,128)(2,1)S(1)} %bitcast.145), channel_id=1, source_target_pairs={{12,0},{0,4},{4,8},{8,12},{13,1},{1,5},{5,9},{9,13},{14,2},{2,6},{... | collective-permute-start | bytes 196616 | tf_op jit(solution)/shard_map/ppermute | solution.py:14
  40.0 11.9 %copy-start.12 = (f32[128]{0:T(128)}, f32[128]{0:T(128)S(1)}, u32[]{:S(2)}) copy-start(f32[128]{0:T(128)S(1)} %fusion.48) | copy-start | bytes 1540
  45.5 4.3 %collective-permute-start.5 = (bf16[128,256]{1,0:T(8,128)(2,1)S(1)}, bf16[128,256]{1,0:T(8,128)(2,1)S(1)}, u32[]{:S(2)}, u32[]{:S(2)}) collective-permute-start(bf16[128,256]{1,0:T(8,128)(2,1)S(1)} %fusion.27), channel_id=1, source_target_pairs={{4,0},{8,4},{12,8},{0,12},{5,1},{9,5},{13,9},{1,13},{6,2},{10,6},{... | collective-permute-start | bytes 196616 | tf_op jit(solution)/shard_map/ppermute | solution.py:14
  45.6 6.3 %collective-permute-start.4 = (bf16[128,256]{1,0:T(8,128)(2,1)S(1)}, bf16[128,256]{1,0:T(8,128)(2,1)S(1)}, u32[]{:S(2)}, u32[]{:S(2)}) collective-permute-start(bf16[128,256]{1,0:T(8,128)(2,1)S(1)} %fusion.27), channel_id=1, source_target_pairs={{12,0},{0,4},{4,8},{8,12},{13,1},{1,5},{5,9},{9,13},{14,2},{2,6},{... | collective-permute-start | bytes 196616 | tf_op jit(solution)/shard_map/ppermute | solution.py:14
  53.4 4.2 %copy-start.6 = (f32[512,256]{1,0:T(8,128)S(1)}, f32[512,256]{1,0:T(8,128)}, u32[]{:S(2)}) copy-start(f32[512,256]{1,0:T(8,128)} %get-tuple-element.25) | copy-start | bytes 1572868
  53.5 4.2 %copy-start.7 = (bf16[1,1,1,512,256]{4,3,2,1,0:T(8,128)(2,1)S(1)}, bf16[1,1,1,512,256]{4,3,2,1,0:T(8,128)(2,1)}, u32[]{:S(2)}) copy-start(bf16[1,1,1,512,256]{4,3,2,1,0:T(8,128)(2,1)} %param.13) | copy-start | bytes 786436
  61.1 10.0 %copy-start.13 = (f32[128]{0:T(128)S(1)}, f32[128]{0:T(128)}, u32[]{:S(2)}) copy-start(f32[128]{0:T(128)} %copy-done.12) | copy-start | bytes 1540
  65.0 6.1 %collective-permute-start.6 = (bf16[128,256]{1,0:T(8,128)(2,1)S(1)}, bf16[128,256]{1,0:T(8,128)(2,1)S(1)}, u32[]{:S(2)}, u32[]{:S(2)}) collective-permute-start(bf16[128,256]{1,0:T(8,128)(2,1)S(1)} %get-tuple-element.20), channel_id=1, source_target_pairs={{12,0},{0,4},{4,8},{8,12},{13,1},{1,5},{5,9},{9,13},{14,2},{2,6},{... | collective-permute-start | bytes 196616 | tf_op jit(solution)/shard_map/ppermute | solution.py:14
  65.0 6.1 %collective-permute-start.7 = (bf16[128,256]{1,0:T(8,128)(2,1)S(1)}, bf16[128,256]{1,0:T(8,128)(2,1)S(1)}, u32[]{:S(2)}, u32[]{:S(2)}) collective-permute-start(bf16[128,256]{1,0:T(8,128)(2,1)S(1)} %get-tuple-element.21), channel_id=1, source_target_pairs={{4,0},{8,4},{12,8},{0,12},{5,1},{9,5},{13,9},{1,13},{6,2},{10,6},{... | collective-permute-start | bytes 196616 | tf_op jit(solution)/shard_map/ppermute | solution.py:14
  71.2 6.1 %collective-permute-start.9 = (bf16[128,256]{1,0:T(8,128)(2,1)S(1)}, bf16[128,256]{1,0:T(8,128)(2,1)S(1)}, u32[]{:S(2)}, u32[]{:S(2)}) collective-permute-start(bf16[128,256]{1,0:T(8,128)(2,1)S(1)} %fusion.30), channel_id=1, source_target_pairs={{4,0},{8,4},{12,8},{0,12},{5,1},{9,5},{13,9},{1,13},{6,2},{10,6},{... | collective-permute-start | bytes 196616 | tf_op jit(solution)/shard_map/ppermute | solution.py:14
  75.4 6.1 %collective-permute-start.8 = (bf16[128,256]{1,0:T(8,128)(2,1)S(1)}, bf16[128,256]{1,0:T(8,128)(2,1)S(1)}, u32[]{:S(2)}, u32[]{:S(2)}) collective-permute-start(bf16[128,256]{1,0:T(8,128)(2,1)S(1)} %fusion.30), channel_id=1, source_target_pairs={{12,0},{0,4},{4,8},{8,12},{13,1},{1,5},{5,9},{9,13},{14,2},{2,6},{... | collective-permute-start | bytes 196616 | tf_op jit(solution)/shard_map/ppermute | solution.py:14
  82.9 3.9 %copy-start.3 = (f32[512,256]{1,0:T(8,128)S(1)}, f32[512,256]{1,0:T(8,128)}, u32[]{:S(2)}) copy-start(f32[512,256]{1,0:T(8,128)} %copy-done.2) | copy-start | bytes 1572868
  (7 other events, 5.7 us)
Sparse Core Ops, SparseCore 0:
  88.9 58.4 reduce-scatter.3
where the time goes:
time: 199 us
  waiting for transfers between devices  68.4 us (34%)
  blocking collectives  50.3 us (25%)
  starting transfers between devices  20.7 us (10%)
  matrix products  20.2 us (10%)
  between operations  14.5 us (7%)
  local copies, waits for them, and re-layouts  12.9 us (6%)
  other arithmetic  11.6 us (6%)
    unnamed x2, waiting for transfers between devices  46.8 us
    all_gather x1, blocking collectives, per_device(): lax.all_gather(weight_part, ('regroup', 'loop'), axis=0, tiled=True)  31.3 us
    ppermute x10, waiting for transfers between devices, shifted(): return lax.ppermute(block, axis, route)  18 us
    ppermute x10, starting transfers between devices, shifted(): return lax.ppermute(block, axis, route)  17.2 us
    psum x1, blocking collectives, per_device(): weight_part = lax.psum(weight_part, 'replica')  11.5 us
    dot_general x2, matrix products, from_nets(): jnp.einsum('tr,tif->rif', row_hot, per_tile, precision=high)  7.83 us
    dot_general x2, matrix products, to_nets(): return jnp.einsum('tc,tjf->cjf', hot, per_tile, precision=high)  7.66 us
    all_to_all x1, blocking collectives, per_device(): lax.all_to_all(grad_rows[None, None], 'regroup', split_axis=3, concat_axi...  7.56 us
  transfers between devices with their start and end apart: 12, of which 9 were waited for; matrix products, arithmetic and copies ran while one was open for 9% of the time, Pallas kernels for 0%

commit v1 on v0

v1 whole, which is shorter than its diff:
```python
import functools
import math

import jax
import jax.numpy as jnp
from jax import lax
from jax.experimental import pallas as pl
from jax.experimental.pallas import tpu as pltpu
from jax.sharding import PartitionSpec as P

EPSILON = 1e-06
MESH = pl.DeviceIdType.MESH
F32 = jnp.float32
BF16 = jnp.bfloat16


def mm(a, b):
    return jnp.dot(a, b, preferred_element_type=F32)


def mm_nt(a, b):
    return lax.dot_general(a, b, (((1,), (1,)), ((), ())), preferred_element_type=F32)


def layer_kernel(
    groups, loops, replicas,
    row_ref, col_ref, width_ref, feat_hbm, weight_ref, tiles_hbm, cot_hbm,
    out_hbm, gf_hbm, gw_ref,
    tiles_ref, cot_ref, x_ref, xt_ref, h_ref, ht_ref, rs_ref, y_ref, q_ref, acc_ref, dpre_ref,
    out_ref, gf_ref, deg_s, deg_r, deinv_ref, part_s, part_r, net_ref, gpart_s, gpart_r, gnet_ref,
    wg_s, wg_r, wz_ref, wf_ref,
    local_sem, feat_ss, feat_rs, deg_ss, deg_rs, part_ss, part_rs, net_ss, net_rs,
    gpart_ss, gpart_rs, gnet_ss, gnet_rs, gf_ss, gf_rs, wg_ss, wg_rs, wz_ss, wz_rs, wf_ss, wf_rs,
):
    slots, edge, _ = tiles_hbm.shape
    cells, chans = cot_hbm.shape
    fw = feat_hbm.shape[1]
    plane = groups * replicas
    my_g = lax.axis_index("regroup")
    my_l = lax.axis_index("loop")
    my_r = lax.axis_index("replica")
    my_p = my_r * groups + my_g

    def group_peer(k):
        return lax.rem(my_g + k, groups)

    def loop_peer(k):
        return lax.rem(my_l + k, loops)

    def plane_peer(k):
        peer = lax.rem(my_p + k, plane)
        return peer, {"replica": lax.div(peer, groups), "regroup": lax.rem(peer, groups)}

    prev_dev = {"loop": loop_peer(loops - 1)}
    next_dev = {"loop": loop_peer(1)}

    def remote(src, dst, ss, rs, dev):
        return pltpu.make_async_remote_copy(
            src_ref=src, dst_ref=dst, send_sem=ss, recv_sem=rs, device_id=dev,
            device_id_type=MESH)

    barrier = pltpu.get_barrier_semaphore()
    for k in range(1, plane):
        pl.semaphore_signal(barrier, inc=1, device_id=plane_peer(k)[1], device_id_type=MESH)
    for k in range(1, loops):
        pl.semaphore_signal(barrier, inc=1, device_id={"loop": loop_peer(k)}, device_id_type=MESH)

    tiles_copy = pltpu.make_async_copy(tiles_hbm, tiles_ref, local_sem.at[0])
    tiles_copy.start()
    own_rows = pl.ds(pl.multiple_of(my_g * cells, cells), cells)
    own_copy = pltpu.make_async_copy(feat_hbm.at[own_rows], x_ref.at[my_g], local_sem.at[1])
    own_copy.start()
    cot_copy = pltpu.make_async_copy(cot_hbm, cot_ref, local_sem.at[2])
    cot_copy.start()

    pl.semaphore_wait(barrier, plane - 1 + loops - 1)

    feat_copies = []
    for k in range(1, groups):
        peer = group_peer(k)
        rows = pl.ds(pl.multiple_of(peer * cells, cells), cells)
        copy = remote(feat_hbm.at[rows], x_ref.at[my_g], feat_ss.at[k], feat_rs.at[k],
                      {"regroup": peer})
        copy.start()
        feat_copies.append(copy)

    tiles_copy.wait()
    half = edge // 2
    lane = lax.broadcasted_iota(jnp.int32, (1, edge), 1)

    def build(rh, carry):
        block = lax.div(rh, 2)
        base = pl.multiple_of(lax.rem(rh, 2) * half, half)

        def add_tile(t, sums):
            tile = tiles_ref[t, pl.ds(base, half), :].astype(F32)
            place = lax.rem(col_ref[t] - my_l + loops, loops)
            live = jnp.where(row_ref[t] == block, width_ref[t], 0)
            spot = jnp.where(place == 0, 1, jnp.where(place == 1, 2, 0))
            new = []
            for c in range(3):
                mask = (lane < jnp.where(spot == c, live, 0)).astype(F32)
                new.append(sums[c] + tile * mask)
            return tuple(new)

        zero = jnp.zeros((half, edge), F32)
        sums = lax.fori_loop(0, slots, add_tile, (zero, zero, zero), unroll=4)
        rows = pl.ds(pl.multiple_of(rh * half, half), half)
        for c in range(3):
            h_ref[rows, c * edge:(c + 1) * edge] = sums[c].astype(BF16)
        return carry

    lax.fori_loop(0, cells // half, build, 0)
    for c in range(3):
        ht_ref[c * edge:(c + 1) * edge, :] = h_ref[:, c * edge:(c + 1) * edge].T

    deg_s[...] = mm(ht_ref[...], jnp.ones((cells, edge), BF16)).astype(BF16).reshape(3, edge, edge)
    deg_copies = [
        remote(deg_s.at[0], deg_r.at[1], deg_ss.at[0], deg_rs.at[1], prev_dev),
        remote(deg_s.at[2], deg_r.at[0], deg_ss.at[1], deg_rs.at[0], next_dev),
    ]
    for copy in deg_copies:
        copy.start()
    rs_ref[...] = lax.rsqrt(1.0 + mm(h_ref[...], jnp.ones((3 * edge, chans), BF16)))

    own_copy.wait()
    for copy in feat_copies:
        copy.wait_recv()
    y32 = mm(x_ref[0], weight_ref[0:fw, :])
    for g in range(1, groups):
        y32 = y32 + mm(x_ref[g], weight_ref[g * fw:(g + 1) * fw, :])
    y16 = y32.astype(BF16)
    y_ref[...] = y16
    q_ref[...] = (y16.astype(F32) * rs_ref[...]).astype(BF16)

    def exchange_sums(send_buf, recv_buf, ss, rs):
        send_buf[0] = mm(ht_ref[0:edge, :], q_ref[...]).astype(BF16)
        down = remote(send_buf.at[0], recv_buf.at[1], ss.at[0], rs.at[1], prev_dev)
        down.start()
        send_buf[1] = mm(ht_ref[2 * edge:, :], q_ref[...]).astype(BF16)
        up = remote(send_buf.at[1], recv_buf.at[0], ss.at[1], rs.at[0], next_dev)
        up.start()
        own = mm(ht_ref[edge:2 * edge, :], q_ref[...]).astype(BF16).astype(F32)
        return own, (down, up)

    def exchange_nets(own, recv_buf, net, ss, rs):
        total = own + recv_buf[0].astype(F32) + recv_buf[1].astype(F32)
        net[1] = (total * deinv_ref[...]).astype(BF16)
        down = remote(net.at[1], net.at[2], ss.at[0], rs.at[1], prev_dev)
        up = remote(net.at[1], net.at[0], ss.at[1], rs.at[0], next_dev)
        down.start()
        up.start()
        acc_ref[...] = mm(h_ref[:, edge:2 * edge], net[1])
        return (down, up)

    own, part_copies = exchange_sums(part_s, part_r, part_ss, part_rs)
    for g in range(groups):
        xt_ref[g * fw:(g + 1) * fw, :] = x_ref[g].T
    for copy in deg_copies:
        copy.wait_recv()
    degree = (1.0 + deg_s[1].astype(F32) + deg_r[0].astype(F32) + deg_r[1].astype(F32))
    inverse = 1.0 / degree
    for c in range(chans // edge):
        deinv_ref[:, c * edge:(c + 1) * edge] = inverse
    for copy in part_copies:
        copy.wait_recv()
    net_copies = exchange_nets(own, part_r, net_ref, net_ss, net_rs)
    cot_copy.wait()
    for copy in net_copies:
        copy.wait_recv()
    acc_ref[...] += mm(h_ref[:, 0:edge], net_ref[0]) + mm(h_ref[:, 2 * edge:], net_ref[2])

    step = 64

    def middle(i, carry):
        rows = pl.ds(pl.multiple_of(i * step, step), step)
        root = rs_ref[rows, :]
        z = acc_ref[rows, :] * root
        inv = lax.rsqrt(jnp.mean(z * z, axis=-1, keepdims=True) + EPSILON)
        normed = z * inv
        pre = y_ref[rows, :].astype(F32) + normed
        sig = 1.0 / (1.0 + jnp.exp(-pre))
        out_ref[rows, :] = (pre * sig).astype(BF16)
        dpre = cot_ref[rows, :].astype(F32) * sig * (1.0 + pre * (1.0 - sig))
        dpre_ref[rows, :] = dpre
        dz = inv * (dpre - normed * jnp.mean(dpre * normed, axis=-1, keepdims=True))
        q_ref[rows, :] = (dz * root).astype(BF16)
        return carry

    lax.fori_loop(0, cells // step, middle, 0)
    out_copy = pltpu.make_async_copy(out_ref, out_hbm, local_sem.at[3])

    own, gpart_copies = exchange_sums(gpart_s, gpart_r, gpart_ss, gpart_rs)
    out_copy.start()
    for copy in gpart_copies:
        copy.wait_recv()
    gnet_copies = exchange_nets(own, gpart_r, gnet_ref, gnet_ss, gnet_rs)
    for copy in gnet_copies:
        copy.wait_recv()
    acc_ref[...] += mm(h_ref[:, 0:edge], gnet_ref[0]) + mm(h_ref[:, 2 * edge:], gnet_ref[2])
    dy = (dpre_ref[...] + acc_ref[...] * rs_ref[...]).astype(BF16)
    q_ref_dy = y_ref
    q_ref_dy[...] = dy

    rows_p = chans // plane
    wg = mm(xt_ref[...], q_ref_dy[...])
    for p in range(plane):
        wg_s[p] = wg[p * rows_p:(p + 1) * rows_p].astype(wg_s.dtype)
    wg_copies = []
    for k in range(1, plane):
        peer, dev = plane_peer(k)
        copy = remote(wg_s.at[peer], wg_r.at[my_p], wg_ss.at[k], wg_rs.at[k], dev)
        copy.start()
        wg_copies.append(copy)
    wg_r[my_p] = wg_s[my_p]

    gf_copies = []
    for k in range(1, groups):
        peer = group_peer(k)
        w_rows = weight_ref[pl.ds(pl.multiple_of(peer * fw, fw), fw), :]
        gf_ref[k] = mm_nt(q_ref_dy[...], w_rows).astype(BF16)
        copy = remote(gf_ref.at[k], gf_hbm.at[own_rows], gf_ss.at[k], gf_rs.at[k],
                      {"regroup": peer})
        copy.start()
        gf_copies.append(copy)
    w_rows = weight_ref[pl.ds(pl.multiple_of(my_g * fw, fw), fw), :]
    gf_ref[0] = mm_nt(q_ref_dy[...], w_rows).astype(BF16)
    gf_own = pltpu.make_async_copy(gf_ref.at[0], gf_hbm.at[own_rows], local_sem.at[4])
    gf_own.start()

    for copy in wg_copies:
        copy.wait_recv()
    piece = wg_r[0].astype(F32)
    for p in range(1, plane):
        piece = piece + wg_r[p].astype(F32)
    wz_ref[my_l] = piece.astype(wz_ref.dtype)
    wz_copies = []
    for k in range(1, loops):
        copy = remote(wz_ref.at[my_l], wz_ref.at[my_l], wz_ss.at[k], wz_rs.at[k],
                      {"loop": loop_peer(k)})
        copy.start()
        wz_copies.append(copy)
    for copy in wz_copies:
        copy.wait_recv()
    piece = wz_ref[0].astype(F32)
    for l in range(1, loops):
        piece = piece + wz_ref[l].astype(F32)
    wf_ref[my_p] = piece.astype(wf_ref.dtype)
    wf_copies = []
    for k in range(1, plane):
        copy = remote(wf_ref.at[my_p], wf_ref.at[my_p], wf_ss.at[k], wf_rs.at[k],
                      plane_peer(k)[1])
        copy.start()
        wf_copies.append(copy)
    for copy in wf_copies:
        copy.wait_recv()
    scale = 1.0 / math.sqrt(cells * plane * loops)
    for p in range(plane):
        gw_ref[p * rows_p:(p + 1) * rows_p, :] = wf_ref[p].astype(F32) * scale

    for copy in gf_copies:
        copy.wait_recv()
    gf_own.wait()
    out_copy.wait()
    for copies in (feat_copies, deg_copies, part_copies, net_copies, gpart_copies, gnet_copies,
                   wg_copies, gf_copies, wz_copies, wf_copies):
        for copy in copies:
            copy.wait_send()


def per_device(groups, loops, replicas,
               features, weight, tiles, tile_row, tile_col, tile_width, cotangent):
    cells, chans = cotangent.shape[-2:]
    slots, edge = tiles.shape[-3:-1]
    total_rows, fw = features.shape[-2:]
    plane = groups * replicas
    rows_p = chans // plane
    link = BF16 if rows_p % 16 == 0 else F32
    smem = pl.BlockSpec(memory_space=pltpu.SMEM)
    vmem = pl.BlockSpec(memory_space=pltpu.VMEM)
    anym = pl.BlockSpec(memory_space=pl.ANY)
    dma = pltpu.SemaphoreType.DMA
    V = pltpu.VMEM
    scratch = [
        V((slots, edge, edge), BF16), V((cells, chans), BF16), V((groups, cells, fw), BF16),
        V((chans, cells), BF16), V((cells, 3 * edge), BF16), V((3 * edge, cells), BF16),
        V((cells, chans), F32), V((cells, chans), BF16), V((cells, chans), BF16),
        V((cells, chans), F32), V((cells, chans), F32), V((cells, chans), BF16),
        V((groups, cells, fw), BF16),
        V((3, edge, edge), BF16), V((2, edge, edge), BF16), V((edge, chans), F32),
        V((2, edge, chans), BF16), V((2, edge, chans), BF16), V((3, edge, chans), BF16),
        V((2, edge, chans), BF16), V((2, edge, chans), BF16), V((3, edge, chans), BF16),
        V((plane, rows_p, chans), link), V((plane, rows_p, chans), link),
        V((loops, rows_p, chans), link), V((plane, rows_p, chans), link),
        dma((5,)), dma((groups,)), dma((groups,)),
        dma((2,)), dma((2,)), dma((2,)), dma((2,)), dma((2,)), dma((2,)),
        dma((2,)), dma((2,)), dma((2,)), dma((2,)), dma((groups,)), dma((groups,)),
        dma((plane,)), dma((plane,)), dma((loops,)), dma((loops,)), dma((plane,)), dma((plane,)),
    ]
    out, gf, gw = pl.pallas_call(
        functools.partial(layer_kernel, groups, loops, replicas),
        out_shape=(
            jax.ShapeDtypeStruct((cells, chans), BF16),
            jax.ShapeDtypeStruct((total_rows, fw), BF16),
            jax.ShapeDtypeStruct((chans, chans), F32),
        ),
        in_specs=[smem, smem, smem, anym, vmem, anym, anym],
        out_specs=(anym, anym, vmem),
        scratch_shapes=scratch,
        compiler_params=pltpu.CompilerParams(
            collective_id=0, has_side_effects=True, vmem_limit_bytes=40 << 20),
    )(tile_row[0, 0, 0], tile_col[0, 0, 0], tile_width[0, 0, 0], features[0, 0], weight,
      tiles[0, 0, 0], cotangent[0, 0, 0])
    return out[None, None, None], gf[None, None], gw


def solution(mesh):
    sizes = dict(mesh.shape)
    return jax.shard_map(
        functools.partial(per_device, sizes["regroup"], sizes["loop"], sizes["replica"]),
        mesh=mesh,
        in_specs=(
            P("replica", "loop", None, "regroup"),
            P(),
            P("replica", "loop", "regroup", None, None, None),
            P("replica", "loop", "regroup", None),
            P("replica", "loop", "regroup", None),
            P("replica", "loop", "regroup", None),
            P("replica", "loop", "regroup", None, None),
        ),
        out_specs=(
            P("replica", "loop", "regroup", None, None),
            P("replica", "loop", None, "regroup"),
            P(),
        ),
        check_vma=False,
    )
```

time: 199 us -> 53.6 us (0.27)
  waiting for transfers between devices: 68.4 us -> 0 us
  blocking collectives: 50.3 us -> 0 us
  Pallas kernels: 0 us -> 45.9 us
  starting transfers between devices: 20.7 us -> 0 us
  matrix products: 20.2 us -> 0 us
  between operations: 14.5 us -> 0.67 us
  other arithmetic: 11.6 us -> 0 us
  local copies, waits for them, and re-layouts: 12.9 us -> 6.8 us
    unnamed x2 -> x0, waiting for transfers between devices: 46.8 us -> none
    pallas_call x0 -> x1, Pallas kernels: none -> 45.9 us  [per_device(): pl.pallas_call(functools.partial(layer_kernel, groups, loops, replicas),...]
    all_gather x1 -> x0, blocking collectives: 31.3 us -> none  [per_device(): lax.all_gather(weight_part, ('regroup', 'loop'), axis=0, tiled=True)]
    dot_general x13 -> x0, matrix products: 20.2 us -> none  [the longest x2 7.83 us: from_nets(): jnp.einsum('tr,tif->rif', row_hot, per_tile, precision=high)]
    ppermute x10 -> x0, waiting for transfers between devices: 18 us -> none  [shifted(): return lax.ppermute(block, axis, route)]
    ppermute x10 -> x0, starting transfers between devices: 17.2 us -> none  [shifted(): return lax.ppermute(block, axis, route)]
    psum x1 -> x0, blocking collectives: 11.5 us -> none  [per_device(): weight_part = lax.psum(weight_part, 'replica')]
    all_to_all x1 -> x0, blocking collectives: 7.56 us -> none  [per_device(): lax.all_to_all(grad_rows[None, None], 'regroup', split_axis=3, concat_axi...]
  transfers between devices with their start and end apart: 12 -> 0, of which waited for: 9 -> 0; matrix products, arithmetic and copies ran while one was open for 9% -> 0% of each run, Pallas kernels for 0% -> 0%
where the time goes in v1:
time: 53.6 us; the launch traced here: 53.3 us
  Pallas kernels  45.9 us (86%)
  local copies, waits for them, and re-layouts  6.8 us (13%)
  between operations  0.67 us (1%)
    pallas_call x1, Pallas kernels, per_device(): pl.pallas_call(functools.partial(layer_kernel, groups, loops, replicas),...  45.9 us
    unnamed x17, local copies, waits for them, and re-layouts  6.8 us

profile of v1, /device:TPU:0, one launch (start us, length us, event | category | flops | bytes accessed | tf_op | source)
XLA Modules:
  0.0 53.3 jit_solution(56640007589072724)
XLA Ops:
  0.6 0.0 copy-start.4
  0.6 0.0 copy-start.5
  0.7 0.0 copy-start.6
  0.7 0.6 %copy-done.4 = s32[1,1,1,32]{3,2,1,0:T(1,128)S(1)} copy-done((s32[1,1,1,32]{3,2,1,0:T(1,128)S(1)}, s32[1,1,1,32]{3,2,1,0:T(1,128)}, u32[]{:S(2)}) %copy-start.4) | copy-done | bytes 152
  1.3 0.0 copy-done.5
  1.3 0.0 copy-done.6
  1.3 0.0 copy-start
  1.3 1.2 %copy-done = bf16[1,1,1,32,128,128]{5,4,3,2,1,0:T(8,128)(2,1)S(1)} copy-done((bf16[1,1,1,32,128,128]{5,4,3,2,1,0:T(8,128)(2,1)S(1)}, bf16[1,1,1,32,128,128]{5,4,3,2,1,0:T(8,128)(2,1)}, u32[]{:S(2)}) %copy-start) | copy-done | bytes 1048600
  2.5 0.0 copy-start.1
  2.5 0.9 %copy-done.1 = bf16[1,1,1024,128]{3,2,1,0:T(8,128)(2,1)S(1)} copy-done((bf16[1,1,1024,128]{3,2,1,0:T(8,128)(2,1)S(1)}, bf16[1,1,1024,128]{3,2,1,0:T(8,128)(2,1)}, u32[]{:S(2)}) %copy-start.1) | copy-done | bytes 262168
  3.5 0.0 copy-start.2
  3.5 0.9 %copy-done.2 = bf16[1,1,1,512,256]{4,3,2,1,0:T(8,128)(2,1)S(1)} copy-done((bf16[1,1,1,512,256]{4,3,2,1,0:T(8,128)(2,1)S(1)}, bf16[1,1,1,512,256]{4,3,2,1,0:T(8,128)(2,1)}, u32[]{:S(2)}) %copy-start.2) | copy-done | bytes 262168
  4.4 0.0 copy-start.3
  4.4 0.9 %copy-done.3 = bf16[256,256]{1,0:T(8,128)(2,1)S(1)} copy-done((bf16[256,256]{1,0:T(8,128)(2,1)S(1)}, bf16[256,256]{1,0:T(8,128)(2,1)}, u32[]{:S(2)}) %copy-start.3) | copy-done | bytes 131096
  5.4 45.9 %shard_map.94 = (bf16[512,256]{1,0:T(8,128)(2,1)S(1)}, bf16[1024,128]{1,0:T(8,128)(2,1)S(1)}, f32[256,256]{1,0:T(8,128)S(1)}) custom-call(s32[32]{0:T(128)S(1)} %bitcast.13, s32[32]{0:T(128)S(1)} %bitcast.14, s32[32]{0:T(128)S(1)} %bitcast.15, bf16[1024,128]{1,0:T(8,128)(2,1)S(1)} %bitcast.11, bf16[256,256]{1,0:T(8,128)(2,1)S(1)} %copy-done.3, ...), custom_call_target="tpu_custom_call" | custom-call | tf_op jit(solution)/shard_map/pallas_call | solution.py:300
  51.2 0.7 %copy.13 = bf16[1,1,1,512,256]{4,3,2,1,0:T(8,128)(2,1)} copy(bf16[1,1,1,512,256]{4,3,2,1,0:T(8,128)(2,1)S(1)} %bitcast.10) | data formatting | bytes 524288
  51.9 0.7 %copy.14 = bf16[1,1,1024,128]{3,2,1,0:T(8,128)(2,1)} copy(bf16[1,1,1024,128]{3,2,1,0:T(8,128)(2,1)S(1)} %bitcast.9) | data formatting | bytes 524288
  52.6 0.7 %copy.15 = f32[256,256]{1,0:T(8,128)} copy(f32[256,256]{1,0:T(8,128)S(1)} %get-tuple-element.14) | data formatting | bytes 524288
Async XLA Ops:
  0.6 0.7 %copy-start.4 = (s32[1,1,1,32]{3,2,1,0:T(1,128)S(1)}, s32[1,1,1,32]{3,2,1,0:T(1,128)}, u32[]{:S(2)}) copy-start(s32[1,1,1,32]{3,2,1,0:T(1,128)} %param.10) | copy-start | bytes 388
  0.6 0.7 %copy-start.5 = (s32[1,1,1,32]{3,2,1,0:T(1,128)S(1)}, s32[1,1,1,32]{3,2,1,0:T(1,128)}, u32[]{:S(2)}) copy-start(s32[1,1,1,32]{3,2,1,0:T(1,128)} %param.11) | copy-start | bytes 388
  0.7 0.7 %copy-start.6 = (s32[1,1,1,32]{3,2,1,0:T(1,128)S(1)}, s32[1,1,1,32]{3,2,1,0:T(1,128)}, u32[]{:S(2)}) copy-start(s32[1,1,1,32]{3,2,1,0:T(1,128)} %param.12) | copy-start | bytes 388
  1.3 1.2 %copy-start = (bf16[1,1,1,32,128,128]{5,4,3,2,1,0:T(8,128)(2,1)S(1)}, bf16[1,1,1,32,128,128]{5,4,3,2,1,0:T(8,128)(2,1)}, u32[]{:S(2)}) copy-start(bf16[1,1,1,32,128,128]{5,4,3,2,1,0:T(8,128)(2,1)} %param.9) | copy-start | bytes 3145732
  2.5 0.9 %copy-start.1 = (bf16[1,1,1024,128]{3,2,1,0:T(8,128)(2,1)S(1)}, bf16[1,1,1024,128]{3,2,1,0:T(8,128)(2,1)}, u32[]{:S(2)}) copy-start(bf16[1,1,1024,128]{3,2,1,0:T(8,128)(2,1)} %param.7) | copy-start | bytes 786436
  3.5 0.9 %copy-start.2 = (bf16[1,1,1,512,256]{4,3,2,1,0:T(8,128)(2,1)S(1)}, bf16[1,1,1,512,256]{4,3,2,1,0:T(8,128)(2,1)}, u32[]{:S(2)}) copy-start(bf16[1,1,1,512,256]{4,3,2,1,0:T(8,128)(2,1)} %param.13) | copy-start | bytes 786436
  4.4 0.9 %copy-start.3 = (bf16[256,256]{1,0:T(8,128)(2,1)S(1)}, bf16[256,256]{1,0:T(8,128)(2,1)}, u32[]{:S(2)}) copy-start(bf16[256,256]{1,0:T(8,128)(2,1)} %weight_ref.1) | copy-start | bytes 393220

commit v2 on v1

--- a/solution.py
+++ b/solution.py
@@ -24,9 +24,9 @@
 
 def layer_kernel(
     groups, loops, replicas,
-    row_ref, col_ref, width_ref, feat_hbm, weight_ref, tiles_hbm, cot_hbm,
-    out_hbm, gf_hbm, gw_ref,
-    tiles_ref, cot_ref, x_ref, xt_ref, h_ref, ht_ref, rs_ref, y_ref, q_ref, acc_ref, dpre_ref,
+    row_hbm, col_hbm, width_hbm, feat_hbm, weight_hbm, tiles_hbm, cot_hbm,
+    out_hbm, gf_out, wf_out,
+    row_ref, col_ref, width_ref, weight_ref, tiles_ref, cot_ref, x_ref, xt_ref, h_ref, ht_ref, rs_ref, y_ref, q_ref, acc_ref, dpre_ref,
     out_ref, gf_ref, deg_s, deg_r, deinv_ref, part_s, part_r, net_ref, gpart_s, gpart_r, gnet_ref,
     wg_s, wg_r, wz_ref, wf_ref,
     local_sem, feat_ss, feat_rs, deg_ss, deg_rs, part_ss, part_rs, net_ss, net_rs,
@@ -65,6 +65,15 @@
     for k in range(1, loops):
         pl.semaphore_signal(barrier, inc=1, device_id={"loop": loop_peer(k)}, device_id_type=MESH)
 
+    index_copies = [
+        pltpu.make_async_copy(src, dst, local_sem.at[5 + i])
+        for i, (src, dst) in enumerate(
+            ((row_hbm, row_ref), (col_hbm, col_ref), (width_hbm, width_ref)))
+    ]
+    for copy in index_copies:
+        copy.start()
+    weight_copy = pltpu.make_async_copy(weight_hbm, weight_ref, local_sem.at[3])
+    weight_copy.start()
     tiles_copy = pltpu.make_async_copy(tiles_hbm, tiles_ref, local_sem.at[0])
     tiles_copy.start()
     own_rows = pl.ds(pl.multiple_of(my_g * cells, cells), cells)
@@ -84,6 +93,8 @@
         copy.start()
         feat_copies.append(copy)
 
+    for copy in index_copies:
+        copy.wait()
     tiles_copy.wait()
     half = edge // 2
     lane = lax.broadcasted_iota(jnp.int32, (1, edge), 1)
@@ -124,6 +135,7 @@
     rs_ref[...] = lax.rsqrt(1.0 + mm(h_ref[...], jnp.ones((3 * edge, chans), BF16)))
 
     own_copy.wait()
+    weight_copy.wait()
     for copy in feat_copies:
         copy.wait_recv()
     y32 = mm(x_ref[0], weight_ref[0:fw, :])
@@ -188,7 +200,7 @@
         return carry
 
     lax.fori_loop(0, cells // step, middle, 0)
-    out_copy = pltpu.make_async_copy(out_ref, out_hbm, local_sem.at[3])
+    out_copy = pltpu.make_async_copy(out_ref, out_hbm, local_sem.at[4])
 
     own, gpart_copies = exchange_sums(gpart_s, gpart_r, gpart_ss, gpart_rs)
     out_copy.start()
@@ -219,13 +231,13 @@
         peer = group_peer(k)
         w_rows = weight_ref[pl.ds(pl.multiple_of(peer * fw, fw), fw), :]
         gf_ref[k] = mm_nt(q_ref_dy[...], w_rows).astype(BF16)
-        copy = remote(gf_ref.at[k], gf_hbm.at[own_rows], gf_ss.at[k], gf_rs.at[k],
+        copy = remote(gf_ref.at[k], gf_out.at[own_rows], gf_ss.at[k], gf_rs.at[k],
                       {"regroup": peer})
         copy.start()
         gf_copies.append(copy)
     w_rows = weight_ref[pl.ds(pl.multiple_of(my_g * fw, fw), fw), :]
     gf_ref[0] = mm_nt(q_ref_dy[...], w_rows).astype(BF16)
-    gf_own = pltpu.make_async_copy(gf_ref.at[0], gf_hbm.at[own_rows], local_sem.at[4])
+    gf_own = pltpu.make_async_copy(gf_ref.at[0], gf_out.at[own_rows], local_sem.at[1])
     gf_own.start()
 
     for copy in wg_copies:
@@ -254,18 +266,36 @@
         wf_copies.append(copy)
     for copy in wf_copies:
         copy.wait_recv()
-    scale = 1.0 / math.sqrt(cells * plane * loops)
-    for p in range(plane):
-        gw_ref[p * rows_p:(p + 1) * rows_p, :] = wf_ref[p].astype(F32) * scale
-
+    wf_copy = pltpu.make_async_copy(wf_ref, wf_out, local_sem.at[0])
+    wf_copy.start()
+    out_copy.wait()
+    gf_own.wait()
+    wf_copy.wait()
     for copy in gf_copies:
         copy.wait_recv()
-    gf_own.wait()
-    out_copy.wait()
     for copies in (feat_copies, deg_copies, part_copies, net_copies, gpart_copies, gnet_copies,
                    wg_copies, gf_copies, wz_copies, wf_copies):
         for copy in copies:
             copy.wait_send()
+
+
+def store_kernel(scale, out_in, gf_in, wf_in, out_hbm, gf_hbm, gw_hbm, wf_ref, gw_ref, sem):
+    load = pltpu.make_async_copy(wf_in, wf_ref, sem.at[3])
+    load.start()
+    copies = [
+        pltpu.make_async_copy(out_in, out_hbm, sem.at[0]),
+        pltpu.make_async_copy(gf_in, gf_hbm, sem.at[1]),
+        pltpu.make_async_copy(gw_ref, gw_hbm, sem.at[2]),
+    ]
+    copies[0].start()
+    copies[1].start()
+    plane, rows_p, _ = wf_ref.shape
+    load.wait()
+    for p in range(plane):
+        gw_ref[p * rows_p:(p + 1) * rows_p, :] = wf_ref[p].astype(F32) * scale
+    copies[2].start()
+    for copy in copies:
+        copy.wait()
 
 
 def per_device(groups, loops, replicas,
@@ -276,41 +306,53 @@
     plane = groups * replicas
     rows_p = chans // plane
     link = BF16 if rows_p % 16 == 0 else F32
-    smem = pl.BlockSpec(memory_space=pltpu.SMEM)
-    vmem = pl.BlockSpec(memory_space=pltpu.VMEM)
     anym = pl.BlockSpec(memory_space=pl.ANY)
     dma = pltpu.SemaphoreType.DMA
     V = pltpu.VMEM
     scratch = [
+        pltpu.SMEM((slots,), jnp.int32), pltpu.SMEM((slots,), jnp.int32),
+        pltpu.SMEM((slots,), jnp.int32), V((chans, chans), BF16),
         V((slots, edge, edge), BF16), V((cells, chans), BF16), V((groups, cells, fw), BF16),
         V((chans, cells), BF16), V((cells, 3 * edge), BF16), V((3 * edge, cells), BF16),
         V((cells, chans), F32), V((cells, chans), BF16), V((cells, chans), BF16),
-        V((cells, chans), F32), V((cells, chans), F32), V((cells, chans), BF16),
-        V((groups, cells, fw), BF16),
+        V((cells, chans), F32), V((cells, chans), F32),
+        V((cells, chans), BF16), V((groups, cells, fw), BF16),
         V((3, edge, edge), BF16), V((2, edge, edge), BF16), V((edge, chans), F32),
         V((2, edge, chans), BF16), V((2, edge, chans), BF16), V((3, edge, chans), BF16),
         V((2, edge, chans), BF16), V((2, edge, chans), BF16), V((3, edge, chans), BF16),
         V((plane, rows_p, chans), link), V((plane, rows_p, chans), link),
         V((loops, rows_p, chans), link), V((plane, rows_p, chans), link),
-        dma((5,)), dma((groups,)), dma((groups,)),
+        dma((8,)), dma((groups,)), dma((groups,)),
         dma((2,)), dma((2,)), dma((2,)), dma((2,)), dma((2,)), dma((2,)),
         dma((2,)), dma((2,)), dma((2,)), dma((2,)), dma((groups,)), dma((groups,)),
         dma((plane,)), dma((plane,)), dma((loops,)), dma((loops,)), dma((plane,)), dma((plane,)),
     ]
+    out, gf, wf = pl.pallas_call(
+        functools.partial(layer_kernel, groups, loops, replicas),
+        out_shape=(
+            jax.ShapeDtypeStruct((cells, chans), BF16),
+            jax.ShapeDtypeStruct((total_rows, fw), BF16),
+            jax.ShapeDtypeStruct((plane, rows_p, chans), link),
+        ),
+        in_specs=[anym] * 7,
+        out_specs=(anym, anym, anym),
+        scratch_shapes=scratch,
+        compiler_params=pltpu.CompilerParams(
+            collective_id=0, has_side_effects=True, vmem_limit_bytes=60 << 20),
+    )(tile_row[0, 0, 0], tile_col[0, 0, 0], tile_width[0, 0, 0], features[0, 0], weight,
+      tiles[0, 0, 0], cotangent[0, 0, 0])
     out, gf, gw = pl.pallas_call(
-        functools.partial(layer_kernel, groups, loops, replicas),
+        functools.partial(store_kernel, 1.0 / math.sqrt(cells * plane * loops)),
         out_shape=(
             jax.ShapeDtypeStruct((cells, chans), BF16),
             jax.ShapeDtypeStruct((total_rows, fw), BF16),
             jax.ShapeDtypeStruct((chans, chans), F32),
         ),
-        in_specs=[smem, smem, smem, anym, vmem, anym, anym],
-        out_specs=(anym, anym, vmem),
-        scratch_shapes=scratch,
-        compiler_params=pltpu.CompilerParams(
-            collective_id=0, has_side_effects=True, vmem_limit_bytes=40 << 20),
-    )(tile_row[0, 0, 0], tile_col[0, 0, 0], tile_width[0, 0, 0], features[0, 0], weight,
-      tiles[0, 0, 0], cotangent[0, 0, 0])
+        in_specs=[anym] * 3,
+        out_specs=(anym, anym, anym),
+        scratch_shapes=[V((plane, rows_p, chans), link), V((chans, chans), F32), dma((4,))],
+        compiler_params=pltpu.CompilerParams(vmem_limit_bytes=60 << 20),
+    )(out, gf, wf)
     return out[None, None, None], gf[None, None], gw
 
 

time: 53.6 us -> 63.7 us (1.19)
  Pallas kernels: 45.9 us -> 62.9 us
  local copies, waits for them, and re-layouts: 6.8 us -> 0 us
    pallas_call x0 -> x1, Pallas kernels: none -> 17 us  [per_device(): pl.pallas_call(functools.partial(store_kernel, 1.0 / math.sqrt(cells * pl...]
    unnamed x17 -> x0, local copies, waits for them, and re-layouts: 6.8 us -> none
where the time goes in v2:
time: 63.7 us; the launch traced here: 63.6 us
  Pallas kernels  62.9 us (99%)
  between operations  0.64 us (1%)
    pallas_call x1, Pallas kernels, per_device(): pl.pallas_call(functools.partial(layer_kernel, groups, loops, replicas),...  45.9 us
    pallas_call x1, Pallas kernels, per_device(): pl.pallas_call(functools.partial(store_kernel, 1.0 / math.sqrt(cells * pl...  17 us

profile of v2, /device:TPU:0, one launch (start us, length us, event | category | flops | bytes accessed | tf_op | source)
XLA Modules:
  0.0 63.6 jit_solution(5665286256660826385)
XLA Ops:
  0.6 45.9 %shard_map.94 = (bf16[512,256]{1,0:T(8,128)(2,1)}, bf16[1024,128]{1,0:T(8,128)(2,1)}, bf16[8,32,256]{2,1,0:T(8,128)(2,1)}) custom-call(s32[32]{0:T(128)} %bitcast.11, s32[32]{0:T(128)} %bitcast.12, s32[32]{0:T(128)} %bitcast.13, bf16[1024,128]{1,0:T(8,128)(2,1)} %bitcast.9, bf16[256,256]{1,0:T(8,128)(2,1)} %weight_hbm.1, bf16[32,128,128]{2,1,0:T(8,128)(2,1)} %bitcast.8, ...), custom_call_target="tpu_custom_call" | custom-call | tf_op jit(solution)/shard_map/pallas_call | solution.py:330
  46.5 17.0 %shard_map.95 = (bf16[512,256]{1,0:T(8,128)(2,1)}, bf16[1024,128]{1,0:T(8,128)(2,1)}, f32[256,256]{1,0:T(8,128)}) custom-call(bf16[512,256]{1,0:T(8,128)(2,1)} %get-tuple-element.9.out_in, bf16[1024,128]{1,0:T(8,128)(2,1)} %get-tuple-element.10.gf_in, bf16[8,32,256]{2,1,0:T(8,128)(2,1)} %get-tuple-element.11.wf_in), custom_call_target="tpu_custom_call" | custom-call | tf_op jit(solution)/shard_map/pallas_call | solution.py:344

commit v3 on v2

--- a/solution.py
+++ b/solution.py
@@ -26,7 +26,7 @@
     groups, loops, replicas,
     row_hbm, col_hbm, width_hbm, feat_hbm, weight_hbm, tiles_hbm, cot_hbm,
     out_hbm, gf_out, wf_out,
-    row_ref, col_ref, width_ref, weight_ref, tiles_ref, cot_ref, x_ref, xt_ref, h_ref, ht_ref, rs_ref, y_ref, q_ref, acc_ref, dpre_ref,
+    row_ref, col_ref, width_ref, weight_ref, tiles_ref, sums_ref, own_ref, cot_ref, x_ref, xt_ref, h_ref, ht_ref, rs_ref, y_ref, q_ref, acc_ref, dpre_ref,
     out_ref, gf_ref, deg_s, deg_r, deinv_ref, part_s, part_r, net_ref, gpart_s, gpart_r, gnet_ref,
     wg_s, wg_r, wz_ref, wf_ref,
     local_sem, feat_ss, feat_rs, deg_ss, deg_rs, part_ss, part_rs, net_ss, net_rs,
@@ -36,6 +36,8 @@
     cells, chans = cot_hbm.shape
     fw = feat_hbm.shape[1]
     plane = groups * replicas
+    width = edge
+    chunks = chans // width
     my_g = lax.axis_index("regroup")
     my_l = lax.axis_index("loop")
     my_r = lax.axis_index("replica")
@@ -96,32 +98,26 @@
     for copy in index_copies:
         copy.wait()
     tiles_copy.wait()
-    half = edge // 2
     lane = lax.broadcasted_iota(jnp.int32, (1, edge), 1)
-
-    def build(rh, carry):
-        block = lax.div(rh, 2)
-        base = pl.multiple_of(lax.rem(rh, 2) * half, half)
-
-        def add_tile(t, sums):
-            tile = tiles_ref[t, pl.ds(base, half), :].astype(F32)
-            place = lax.rem(col_ref[t] - my_l + loops, loops)
-            live = jnp.where(row_ref[t] == block, width_ref[t], 0)
-            spot = jnp.where(place == 0, 1, jnp.where(place == 1, 2, 0))
-            new = []
-            for c in range(3):
-                mask = (lane < jnp.where(spot == c, live, 0)).astype(F32)
-                new.append(sums[c] + tile * mask)
-            return tuple(new)
-
-        zero = jnp.zeros((half, edge), F32)
-        sums = lax.fori_loop(0, slots, add_tile, (zero, zero, zero), unroll=4)
-        rows = pl.ds(pl.multiple_of(rh * half, half), half)
+    blocks = cells // edge
+    spots = 3 * blocks
+    sums_ref[0] = jnp.zeros((edge, edge), F32)
+
+    def add_tile(t, last):
+        place = lax.rem(col_ref[t] - my_l + loops, loops)
+        spot = row_ref[t] * 3 + jnp.where(place == 0, 1, jnp.where(place == 1, 2, 0))
+        link = jnp.int32(0)
+        for k in range(spots):
+            link = jnp.where(spot == k, last[k], link)
+        tile = jnp.where(lane < width_ref[t], tiles_ref[t].astype(F32), 0.0)
+        sums_ref[t + 1] = tile + sums_ref[link]
+        return tuple(jnp.where(spot == k, t + 1, last[k]) for k in range(spots))
+
+    last = lax.fori_loop(0, slots, add_tile, (jnp.int32(0),) * spots, unroll=4)
+    for b in range(blocks):
         for c in range(3):
-            h_ref[rows, c * edge:(c + 1) * edge] = sums[c].astype(BF16)
-        return carry
-
-    lax.fori_loop(0, cells // half, build, 0)
+            h_ref[b * edge:(b + 1) * edge, c * edge:(c + 1) * edge] = (
+                sums_ref[last[b * 3 + c]].astype(BF16))
     for c in range(3):
         ht_ref[c * edge:(c + 1) * edge, :] = h_ref[:, c * edge:(c + 1) * edge].T
 
@@ -145,42 +141,55 @@
     y_ref[...] = y16
     q_ref[...] = (y16.astype(F32) * rs_ref[...]).astype(BF16)
 
-    def exchange_sums(send_buf, recv_buf, ss, rs):
-        send_buf[0] = mm(ht_ref[0:edge, :], q_ref[...]).astype(BF16)
-        down = remote(send_buf.at[0], recv_buf.at[1], ss.at[0], rs.at[1], prev_dev)
-        down.start()
-        send_buf[1] = mm(ht_ref[2 * edge:, :], q_ref[...]).astype(BF16)
-        up = remote(send_buf.at[1], recv_buf.at[0], ss.at[1], rs.at[0], next_dev)
-        up.start()
-        own = mm(ht_ref[edge:2 * edge, :], q_ref[...]).astype(BF16).astype(F32)
-        return own, (down, up)
-
-    def exchange_nets(own, recv_buf, net, ss, rs):
-        total = own + recv_buf[0].astype(F32) + recv_buf[1].astype(F32)
-        net[1] = (total * deinv_ref[...]).astype(BF16)
-        down = remote(net.at[1], net.at[2], ss.at[0], rs.at[1], prev_dev)
-        up = remote(net.at[1], net.at[0], ss.at[1], rs.at[0], next_dev)
-        down.start()
-        up.start()
-        acc_ref[...] = mm(h_ref[:, edge:2 * edge], net[1])
-        return (down, up)
-
-    own, part_copies = exchange_sums(part_s, part_r, part_ss, part_rs)
+    def start_sums(send_buf, recv_buf, ss, rs):
+        owns, copies = [], []
+        for h in range(chunks):
+            sums = mm(ht_ref[...], q_ref[:, h * width:(h + 1) * width])
+            send_buf[h, 0] = sums[0:edge].astype(BF16)
+            send_buf[h, 1] = sums[2 * edge:].astype(BF16)
+            pair = (
+                remote(send_buf.at[h, 0], recv_buf.at[h, 1], ss.at[h, 0], rs.at[h, 1], prev_dev),
+                remote(send_buf.at[h, 1], recv_buf.at[h, 0], ss.at[h, 1], rs.at[h, 0], next_dev),
+            )
+            for copy in pair:
+                copy.start()
+            copies.append(pair)
+            own_ref[:, h * width:(h + 1) * width] = sums[edge:2 * edge].astype(BF16)
+        return copies
+
+    def start_nets(copies, recv_buf, net, ss, rs):
+        news = []
+        for h in range(chunks):
+            for copy in copies[h]:
+                copy.wait_recv()
+            total = (own_ref[:, h * width:(h + 1) * width].astype(F32)
+                     + recv_buf[h, 0].astype(F32) + recv_buf[h, 1].astype(F32))
+            net[h, 1] = (total * deinv_ref[:, 0:width]).astype(BF16)
+            pair = (
+                remote(net.at[h, 1], net.at[h, 2], ss.at[h, 0], rs.at[h, 1], prev_dev),
+                remote(net.at[h, 1], net.at[h, 0], ss.at[h, 1], rs.at[h, 0], next_dev),
+            )
+            for copy in pair:
+                copy.start()
+            news.append(pair)
+        return news
+
+    def finish_nets(copies, net, h):
+        for copy in copies[h]:
+            copy.wait_recv()
+        return mm(h_ref[...], net[h].reshape(3 * edge, width))
+
+    part_copies = start_sums(part_s, part_r, part_ss, part_rs)
     for g in range(groups):
         xt_ref[g * fw:(g + 1) * fw, :] = x_ref[g].T
     for copy in deg_copies:
         copy.wait_recv()
     degree = (1.0 + deg_s[1].astype(F32) + deg_r[0].astype(F32) + deg_r[1].astype(F32))
-    inverse = 1.0 / degree
-    for c in range(chans // edge):
-        deinv_ref[:, c * edge:(c + 1) * edge] = inverse
-    for copy in part_copies:
-        copy.wait_recv()
-    net_copies = exchange_nets(own, part_r, net_ref, net_ss, net_rs)
+    deinv_ref[...] = 1.0 / degree
+    net_copies = start_nets(part_copies, part_r, net_ref, net_ss, net_rs)
     cot_copy.wait()
-    for copy in net_copies:
-        copy.wait_recv()
-    acc_ref[...] += mm(h_ref[:, 0:edge], net_ref[0]) + mm(h_ref[:, 2 * edge:], net_ref[2])
+    for h in range(chunks):
+        acc_ref[:, h * width:(h + 1) * width] = finish_nets(net_copies, net_ref, h)
 
     step = 64
 
@@ -199,59 +208,56 @@
         q_ref[rows, :] = (dz * root).astype(BF16)
         return carry
 
-    lax.fori_loop(0, cells // step, middle, 0)
+    lax.fori_loop(0, cells // step, middle, 0, unroll=2)
     out_copy = pltpu.make_async_copy(out_ref, out_hbm, local_sem.at[4])
 
-    own, gpart_copies = exchange_sums(gpart_s, gpart_r, gpart_ss, gpart_rs)
+    gpart_copies = start_sums(gpart_s, gpart_r, gpart_ss, gpart_rs)
     out_copy.start()
-    for copy in gpart_copies:
-        copy.wait_recv()
-    gnet_copies = exchange_nets(own, gpart_r, gnet_ref, gnet_ss, gnet_rs)
-    for copy in gnet_copies:
-        copy.wait_recv()
-    acc_ref[...] += mm(h_ref[:, 0:edge], gnet_ref[0]) + mm(h_ref[:, 2 * edge:], gnet_ref[2])
-    dy = (dpre_ref[...] + acc_ref[...] * rs_ref[...]).astype(BF16)
-    q_ref_dy = y_ref
-    q_ref_dy[...] = dy
+    gnet_copies = start_nets(gpart_copies, gpart_r, gnet_ref, gnet_ss, gnet_rs)
 
     rows_p = chans // plane
-    wg = mm(xt_ref[...], q_ref_dy[...])
-    for p in range(plane):
-        wg_s[p] = wg[p * rows_p:(p + 1) * rows_p].astype(wg_s.dtype)
     wg_copies = []
-    for k in range(1, plane):
-        peer, dev = plane_peer(k)
-        copy = remote(wg_s.at[peer], wg_r.at[my_p], wg_ss.at[k], wg_rs.at[k], dev)
-        copy.start()
-        wg_copies.append(copy)
-    wg_r[my_p] = wg_s[my_p]
+    for h in range(chunks):
+        cols = slice(h * width, (h + 1) * width)
+        back = finish_nets(gnet_copies, gnet_ref, h)
+        dy = (dpre_ref[:, cols] + back * rs_ref[:, cols]).astype(BF16)
+        y_ref[:, cols] = dy
+        wg = mm(xt_ref[...], dy)
+        for p in range(plane):
+            wg_s[h, p] = wg[p * rows_p:(p + 1) * rows_p].astype(wg_s.dtype)
+        for k in range(1, plane):
+            peer, dev = plane_peer(k)
+            copy = remote(wg_s.at[h, peer], wg_r.at[h, my_p], wg_ss.at[h, k], wg_rs.at[h, k], dev)
+            copy.start()
+            wg_copies.append(copy)
+        wg_r[h, my_p] = wg_s[h, my_p]
 
     gf_copies = []
-    for k in range(1, groups):
+    for k in range(groups):
         peer = group_peer(k)
         w_rows = weight_ref[pl.ds(pl.multiple_of(peer * fw, fw), fw), :]
-        gf_ref[k] = mm_nt(q_ref_dy[...], w_rows).astype(BF16)
-        copy = remote(gf_ref.at[k], gf_out.at[own_rows], gf_ss.at[k], gf_rs.at[k],
-                      {"regroup": peer})
-        copy.start()
-        gf_copies.append(copy)
-    w_rows = weight_ref[pl.ds(pl.multiple_of(my_g * fw, fw), fw), :]
-    gf_ref[0] = mm_nt(q_ref_dy[...], w_rows).astype(BF16)
+        gf_ref[k] = mm_nt(y_ref[...], w_rows).astype(BF16)
+        if k > 0:
+            gf_copies.append(remote(gf_ref.at[k], gf_out.at[own_rows], gf_ss.at[k], gf_rs.at[k],
+                                    {"regroup": peer}))
     gf_own = pltpu.make_async_copy(gf_ref.at[0], gf_out.at[own_rows], local_sem.at[1])
     gf_own.start()
 
     for copy in wg_copies:
         copy.wait_recv()
-    piece = wg_r[0].astype(F32)
-    for p in range(1, plane):
-        piece = piece + wg_r[p].astype(F32)
-    wz_ref[my_l] = piece.astype(wz_ref.dtype)
+    for h in range(chunks):
+        piece = wg_r[h, 0].astype(F32)
+        for p in range(1, plane):
+            piece = piece + wg_r[h, p].astype(F32)
+        wz_ref[my_l, :, h * width:(h + 1) * width] = piece.astype(wz_ref.dtype)
     wz_copies = []
     for k in range(1, loops):
         copy = remote(wz_ref.at[my_l], wz_ref.at[my_l], wz_ss.at[k], wz_rs.at[k],
                       {"loop": loop_peer(k)})
         copy.start()
         wz_copies.append(copy)
+    for copy in gf_copies:
+        copy.start()
     for copy in wz_copies:
         copy.wait_recv()
     piece = wz_ref[0].astype(F32)
@@ -273,29 +279,35 @@
     wf_copy.wait()
     for copy in gf_copies:
         copy.wait_recv()
-    for copies in (feat_copies, deg_copies, part_copies, net_copies, gpart_copies, gnet_copies,
-                   wg_copies, gf_copies, wz_copies, wf_copies):
+    for copies in (feat_copies, deg_copies, wg_copies, gf_copies, wz_copies, wf_copies,
+                   *part_copies, *net_copies, *gpart_copies, *gnet_copies):
         for copy in copies:
             copy.wait_send()
 
 
-def store_kernel(scale, out_in, gf_in, wf_in, out_hbm, gf_hbm, gw_hbm, wf_ref, gw_ref, sem):
-    load = pltpu.make_async_copy(wf_in, wf_ref, sem.at[3])
-    load.start()
-    copies = [
-        pltpu.make_async_copy(out_in, out_hbm, sem.at[0]),
-        pltpu.make_async_copy(gf_in, gf_hbm, sem.at[1]),
+def store_kernel(scale, out_in, gf_in, wf_in, out_hbm, gf_hbm, gw_hbm,
+                 out_ref, gf_ref, wf_ref, gw_ref, sem):
+    loads = [
+        pltpu.make_async_copy(out_in, out_ref, sem.at[3]),
+        pltpu.make_async_copy(gf_in, gf_ref, sem.at[4]),
+        pltpu.make_async_copy(wf_in, wf_ref, sem.at[5]),
+    ]
+    stores = [
+        pltpu.make_async_copy(out_ref, out_hbm, sem.at[0]),
+        pltpu.make_async_copy(gf_ref, gf_hbm, sem.at[1]),
         pltpu.make_async_copy(gw_ref, gw_hbm, sem.at[2]),
     ]
-    copies[0].start()
-    copies[1].start()
+    for load in loads:
+        load.start()
     plane, rows_p, _ = wf_ref.shape
-    load.wait()
-    for p in range(plane):
-        gw_ref[p * rows_p:(p + 1) * rows_p, :] = wf_ref[p].astype(F32) * scale
-    copies[2].start()
-    for copy in copies:
-        copy.wait()
+    for load, store in zip(loads, stores):
+        load.wait()
+        if store is stores[2]:
+            for p in range(plane):
+                gw_ref[p * rows_p:(p + 1) * rows_p, :] = wf_ref[p].astype(F32) * scale
+        store.start()
+    for store in stores:
+        store.wait()
 
 
 def per_device(groups, loops, replicas,
@@ -305,6 +317,7 @@
     total_rows, fw = features.shape[-2:]
     plane = groups * replicas
     rows_p = chans // plane
+    chunks = chans // edge
     link = BF16 if rows_p % 16 == 0 else F32
     anym = pl.BlockSpec(memory_space=pl.ANY)
     dma = pltpu.SemaphoreType.DMA
@@ -312,20 +325,20 @@
     scratch = [
         pltpu.SMEM((slots,), jnp.int32), pltpu.SMEM((slots,), jnp.int32),
         pltpu.SMEM((slots,), jnp.int32), V((chans, chans), BF16),
-        V((slots, edge, edge), BF16), V((cells, chans), BF16), V((groups, cells, fw), BF16),
+        V((slots, edge, edge), BF16), V((slots + 1, edge, edge), F32), V((edge, chans), BF16),
+        V((cells, chans), BF16), V((groups, cells, fw), BF16),
         V((chans, cells), BF16), V((cells, 3 * edge), BF16), V((3 * edge, cells), BF16),
         V((cells, chans), F32), V((cells, chans), BF16), V((cells, chans), BF16),
         V((cells, chans), F32), V((cells, chans), F32),
         V((cells, chans), BF16), V((groups, cells, fw), BF16),
-        V((3, edge, edge), BF16), V((2, edge, edge), BF16), V((edge, chans), F32),
-        V((2, edge, chans), BF16), V((2, edge, chans), BF16), V((3, edge, chans), BF16),
-        V((2, edge, chans), BF16), V((2, edge, chans), BF16), V((3, edge, chans), BF16),
-        V((plane, rows_p, chans), link), V((plane, rows_p, chans), link),
+        V((3, edge, edge), BF16), V((2, edge, edge), BF16), V((edge, edge), F32),
+        *([V((chunks, 2, edge, edge), BF16)] * 2), V((chunks, 3, edge, edge), BF16),
+        *([V((chunks, 2, edge, edge), BF16)] * 2), V((chunks, 3, edge, edge), BF16),
+        *([V((chunks, plane, rows_p, edge), link)] * 2),
         V((loops, rows_p, chans), link), V((plane, rows_p, chans), link),
-        dma((8,)), dma((groups,)), dma((groups,)),
-        dma((2,)), dma((2,)), dma((2,)), dma((2,)), dma((2,)), dma((2,)),
-        dma((2,)), dma((2,)), dma((2,)), dma((2,)), dma((groups,)), dma((groups,)),
-        dma((plane,)), dma((plane,)), dma((loops,)), dma((loops,)), dma((plane,)), dma((plane,)),
+        dma((8,)), dma((groups,)), dma((groups,)), dma((2,)), dma((2,)),
+        *([dma((chunks, 2))] * 8), dma((groups,)), dma((groups,)),
+        *([dma((chunks, plane))] * 2), *([dma((loops,))] * 2), *([dma((plane,))] * 2),
     ]
     out, gf, wf = pl.pallas_call(
         functools.partial(layer_kernel, groups, loops, replicas),
@@ -350,7 +363,10 @@
         ),
         in_specs=[anym] * 3,
         out_specs=(anym, anym, anym),
-        scratch_shapes=[V((plane, rows_p, chans), link), V((chans, chans), F32), dma((4,))],
+        scratch_shapes=[
+            V((cells, chans), BF16), V((total_rows, fw), BF16), V((plane, rows_p, chans), link),
+            V((chans, chans), F32), dma((6,)),
+        ],
         compiler_params=pltpu.CompilerParams(vmem_limit_bytes=60 << 20),
     )(out, gf, wf)
     return out[None, None, None], gf[None, None], gw

time: 63.7 us -> 46.8 us (0.73)
  Pallas kernels: 62.9 us -> 46 us
    pallas_call x1, Pallas kernels: 17 us -> 1.88 us  [per_device(): pl.pallas_call(functools.partial(store_kernel, 1.0 / math.sqrt(cells * pl...]
    pallas_call x1, Pallas kernels: 45.9 us -> 44.1 us  [per_device(): pl.pallas_call(functools.partial(layer_kernel, groups, loops, replicas),...]
where the time goes in v3:
time: 46.8 us; the launch traced here: 46.6 us
  Pallas kernels  46 us (98%)
  between operations  0.64 us (1%)
    pallas_call x1, Pallas kernels, per_device(): pl.pallas_call(functools.partial(layer_kernel, groups, loops, replicas),...  44.1 us
    pallas_call x1, Pallas kernels, per_device(): pl.pallas_call(functools.partial(store_kernel, 1.0 / math.sqrt(cells * pl...  1.88 us

profile of v3, /device:TPU:0, one launch (start us, length us, event | category | flops | bytes accessed | tf_op | source)
XLA Modules:
  0.0 46.6 jit_solution(8585941542375441503)
XLA Ops:
  0.6 44.1 %shard_map.94 = (bf16[512,256]{1,0:T(8,128)(2,1)}, bf16[1024,128]{1,0:T(8,128)(2,1)}, bf16[8,32,256]{2,1,0:T(8,128)(2,1)}) custom-call(s32[32]{0:T(128)} %bitcast.11, s32[32]{0:T(128)} %bitcast.12, s32[32]{0:T(128)} %bitcast.13, bf16[1024,128]{1,0:T(8,128)(2,1)} %bitcast.9, bf16[256,256]{1,0:T(8,128)(2,1)} %weight_hbm.1, bf16[32,128,128]{2,1,0:T(8,128)(2,1)} %bitcast.8, ...), custom_call_target="tpu_custom_call" | custom-call | tf_op jit(solution)/shard_map/pallas_call | solution.py:343
  44.8 1.9 %shard_map.95 = (bf16[512,256]{1,0:T(8,128)(2,1)}, bf16[1024,128]{1,0:T(8,128)(2,1)}, f32[256,256]{1,0:T(8,128)}) custom-call(bf16[512,256]{1,0:T(8,128)(2,1)} %get-tuple-element.9.out_in, bf16[1024,128]{1,0:T(8,128)(2,1)} %get-tuple-element.10.gf_in, bf16[8,32,256]{2,1,0:T(8,128)(2,1)} %get-tuple-element.11.wf_in), custom_call_target="tpu_custom_call" | custom-call | tf_op jit(solution)/shard_map/pallas_call | solution.py:357

commit v4 on v3

--- a/solution.py
+++ b/solution.py
@@ -26,7 +26,7 @@
     groups, loops, replicas,
     row_hbm, col_hbm, width_hbm, feat_hbm, weight_hbm, tiles_hbm, cot_hbm,
     out_hbm, gf_out, wf_out,
-    row_ref, col_ref, width_ref, weight_ref, tiles_ref, sums_ref, own_ref, cot_ref, x_ref, xt_ref, h_ref, ht_ref, rs_ref, y_ref, q_ref, acc_ref, dpre_ref,
+    row_ref, col_ref, width_ref, weight_ref, tiles_ref, sums_ref, own_ref, usum_ref, ut_ref, direct_ref, cot_ref, x_ref, xt_ref, h_ref, ht_ref, rs_ref, y_ref, q_ref, acc_ref, dpre_ref,
     out_ref, gf_ref, deg_s, deg_r, deinv_ref, part_s, part_r, net_ref, gpart_s, gpart_r, gnet_ref,
     wg_s, wg_r, wz_ref, wf_ref,
     local_sem, feat_ss, feat_rs, deg_ss, deg_rs, part_ss, part_rs, net_ss, net_rs,
@@ -130,63 +130,77 @@
         copy.start()
     rs_ref[...] = lax.rsqrt(1.0 + mm(h_ref[...], jnp.ones((3 * edge, chans), BF16)))
 
+    weight_copy.wait()
     own_copy.wait()
-    weight_copy.wait()
-    for copy in feat_copies:
-        copy.wait_recv()
+
+    def group_rows(k):
+        source = lax.rem(my_g + groups - k, groups)
+        return source, pl.ds(pl.multiple_of(source * fw, fw), fw)
+
+    def send_sums(sums, send, recv, ss, rs):
+        send[0] = sums[0:edge].astype(BF16)
+        send[1] = sums[2 * edge:].astype(BF16)
+        pair = (
+            remote(send.at[0], recv.at[1], ss.at[0], rs.at[1], prev_dev),
+            remote(send.at[1], recv.at[0], ss.at[1], rs.at[0], next_dev),
+        )
+        for copy in pair:
+            copy.start()
+        return pair
+
+    part_copies = []
+    for k in range(groups):
+        source, _ = group_rows(k)
+        if k > 0:
+            feat_copies[k - 1].wait_recv()
+        xs = (x_ref[source].astype(F32) * rs_ref[:, 0:fw]).astype(BF16)
+        sums = mm(ht_ref[...], xs)
+        part_copies.append(send_sums(
+            sums, part_s.at[k], part_r.at[k], part_ss.at[k], part_rs.at[k]))
+        usum_ref[k] = sums[edge:2 * edge].astype(BF16)
+
     y32 = mm(x_ref[0], weight_ref[0:fw, :])
     for g in range(1, groups):
         y32 = y32 + mm(x_ref[g], weight_ref[g * fw:(g + 1) * fw, :])
-    y16 = y32.astype(BF16)
-    y_ref[...] = y16
-    q_ref[...] = (y16.astype(F32) * rs_ref[...]).astype(BF16)
-
-    def start_sums(send_buf, recv_buf, ss, rs):
-        owns, copies = [], []
-        for h in range(chunks):
-            sums = mm(ht_ref[...], q_ref[:, h * width:(h + 1) * width])
-            send_buf[h, 0] = sums[0:edge].astype(BF16)
-            send_buf[h, 1] = sums[2 * edge:].astype(BF16)
-            pair = (
-                remote(send_buf.at[h, 0], recv_buf.at[h, 1], ss.at[h, 0], rs.at[h, 1], prev_dev),
-                remote(send_buf.at[h, 1], recv_buf.at[h, 0], ss.at[h, 1], rs.at[h, 0], next_dev),
-            )
-            for copy in pair:
-                copy.start()
-            copies.append(pair)
-            own_ref[:, h * width:(h + 1) * width] = sums[edge:2 * edge].astype(BF16)
-        return copies
-
-    def start_nets(copies, recv_buf, net, ss, rs):
-        news = []
-        for h in range(chunks):
-            for copy in copies[h]:
-                copy.wait_recv()
-            total = (own_ref[:, h * width:(h + 1) * width].astype(F32)
-                     + recv_buf[h, 0].astype(F32) + recv_buf[h, 1].astype(F32))
-            net[h, 1] = (total * deinv_ref[:, 0:width]).astype(BF16)
-            pair = (
-                remote(net.at[h, 1], net.at[h, 2], ss.at[h, 0], rs.at[h, 1], prev_dev),
-                remote(net.at[h, 1], net.at[h, 0], ss.at[h, 1], rs.at[h, 0], next_dev),
-            )
-            for copy in pair:
-                copy.start()
-            news.append(pair)
-        return news
+    y_ref[...] = y32.astype(BF16)
+
+    def send_nets(net, ss, rs):
+        pair = (
+            remote(net.at[1], net.at[2], ss.at[0], rs.at[1], prev_dev),
+            remote(net.at[1], net.at[0], ss.at[1], rs.at[0], next_dev),
+        )
+        for copy in pair:
+            copy.start()
+        return pair
 
     def finish_nets(copies, net, h):
         for copy in copies[h]:
             copy.wait_recv()
         return mm(h_ref[...], net[h].reshape(3 * edge, width))
 
-    part_copies = start_sums(part_s, part_r, part_ss, part_rs)
     for g in range(groups):
         xt_ref[g * fw:(g + 1) * fw, :] = x_ref[g].T
     for copy in deg_copies:
         copy.wait_recv()
     degree = (1.0 + deg_s[1].astype(F32) + deg_r[0].astype(F32) + deg_r[1].astype(F32))
     deinv_ref[...] = 1.0 / degree
-    net_copies = start_nets(part_copies, part_r, net_ref, net_ss, net_rs)
+    nets = None
+    for k in range(groups):
+        _, rows = group_rows(k)
+        for copy in part_copies[k]:
+            copy.wait_recv()
+        total = (usum_ref[k].astype(F32) + part_r[k, 0].astype(F32) + part_r[k, 1].astype(F32)
+                 ).astype(BF16)
+        usum_ref[k] = total
+        term = mm(total, weight_ref[rows, :])
+        nets = term if nets is None else nets + term
+    net_copies = []
+    for h in range(chunks):
+        net_ref[h, 1] = (nets[:, h * width:(h + 1) * width] * deinv_ref[...]).astype(BF16)
+        net_copies.append(send_nets(net_ref.at[h], net_ss.at[h], net_rs.at[h]))
+    for k in range(groups):
+        _, rows = group_rows(k)
+        ut_ref[rows, :] = usum_ref[k].T
     cot_copy.wait()
     for h in range(chunks):
         acc_ref[:, h * width:(h + 1) * width] = finish_nets(net_copies, net_ref, h)
@@ -211,18 +225,27 @@
     lax.fori_loop(0, cells // step, middle, 0, unroll=2)
     out_copy = pltpu.make_async_copy(out_ref, out_hbm, local_sem.at[4])
 
-    gpart_copies = start_sums(gpart_s, gpart_r, gpart_ss, gpart_rs)
-    out_copy.start()
-    gnet_copies = start_nets(gpart_copies, gpart_r, gnet_ref, gnet_ss, gnet_rs)
-
-    rows_p = chans // plane
-    wg_copies = []
+    gpart_copies = []
     for h in range(chunks):
         cols = slice(h * width, (h + 1) * width)
-        back = finish_nets(gnet_copies, gnet_ref, h)
-        dy = (dpre_ref[:, cols] + back * rs_ref[:, cols]).astype(BF16)
-        y_ref[:, cols] = dy
-        wg = mm(xt_ref[...], dy)
+        sums = mm(ht_ref[...], q_ref[:, cols])
+        gpart_copies.append(send_sums(
+            sums, gpart_s.at[h], gpart_r.at[h], gpart_ss.at[h], gpart_rs.at[h]))
+        own_ref[:, cols] = sums[edge:2 * edge].astype(BF16)
+    out_copy.start()
+
+    rows_p = chans // plane
+    direct_ref[...] = mm(xt_ref[...], dpre_ref[...].astype(BF16))
+    gnet_copies, wg_copies = [], []
+    for h in range(chunks):
+        cols = slice(h * width, (h + 1) * width)
+        for copy in gpart_copies[h]:
+            copy.wait_recv()
+        total = (own_ref[:, cols].astype(F32)
+                 + gpart_r[h, 0].astype(F32) + gpart_r[h, 1].astype(F32))
+        gnet_ref[h, 1] = (total * deinv_ref[...]).astype(BF16)
+        gnet_copies.append(send_nets(gnet_ref.at[h], gnet_ss.at[h], gnet_rs.at[h]))
+        wg = direct_ref[:, cols] + mm(ut_ref[...], gnet_ref[h, 1])
         for p in range(plane):
             wg_s[h, p] = wg[p * rows_p:(p + 1) * rows_p].astype(wg_s.dtype)
         for k in range(1, plane):
@@ -232,16 +255,13 @@
             wg_copies.append(copy)
         wg_r[h, my_p] = wg_s[h, my_p]
 
-    gf_copies = []
-    for k in range(groups):
-        peer = group_peer(k)
-        w_rows = weight_ref[pl.ds(pl.multiple_of(peer * fw, fw), fw), :]
-        gf_ref[k] = mm_nt(y_ref[...], w_rows).astype(BF16)
-        if k > 0:
-            gf_copies.append(remote(gf_ref.at[k], gf_out.at[own_rows], gf_ss.at[k], gf_rs.at[k],
-                                    {"regroup": peer}))
-    gf_own = pltpu.make_async_copy(gf_ref.at[0], gf_out.at[own_rows], local_sem.at[1])
-    gf_own.start()
+    def finish_grad(h):
+        cols = slice(h * width, (h + 1) * width)
+        back = finish_nets(gnet_copies, gnet_ref, h)
+        y_ref[:, cols] = (dpre_ref[:, cols] + back * rs_ref[:, cols]).astype(BF16)
+
+    for h in range(chunks - 1):
+        finish_grad(h)
 
     for copy in wg_copies:
         copy.wait_recv()
@@ -256,8 +276,20 @@
                       {"loop": loop_peer(k)})
         copy.start()
         wz_copies.append(copy)
-    for copy in gf_copies:
-        copy.start()
+    finish_grad(chunks - 1)
+    gf_copies = []
+    for k in [*range(1, groups), 0]:
+        peer = group_peer(k)
+        w_rows = weight_ref[pl.ds(pl.multiple_of(peer * fw, fw), fw), :]
+        gf_ref[k] = mm_nt(y_ref[...], w_rows).astype(BF16)
+        if k > 0:
+            copy = remote(gf_ref.at[k], gf_out.at[own_rows], gf_ss.at[k], gf_rs.at[k],
+                          {"regroup": peer})
+            copy.start()
+            gf_copies.append(copy)
+    gf_own = pltpu.make_async_copy(gf_ref.at[0], gf_out.at[own_rows], local_sem.at[1])
+    gf_own.start()
+
     for copy in wz_copies:
         copy.wait_recv()
     piece = wz_ref[0].astype(F32)
@@ -326,18 +358,19 @@
         pltpu.SMEM((slots,), jnp.int32), pltpu.SMEM((slots,), jnp.int32),
         pltpu.SMEM((slots,), jnp.int32), V((chans, chans), BF16),
         V((slots, edge, edge), BF16), V((slots + 1, edge, edge), F32), V((edge, chans), BF16),
+        V((groups, edge, fw), BF16), V((chans, edge), BF16), V((chans, chans), F32),
         V((cells, chans), BF16), V((groups, cells, fw), BF16),
         V((chans, cells), BF16), V((cells, 3 * edge), BF16), V((3 * edge, cells), BF16),
         V((cells, chans), F32), V((cells, chans), BF16), V((cells, chans), BF16),
         V((cells, chans), F32), V((cells, chans), F32),
         V((cells, chans), BF16), V((groups, cells, fw), BF16),
         V((3, edge, edge), BF16), V((2, edge, edge), BF16), V((edge, edge), F32),
-        *([V((chunks, 2, edge, edge), BF16)] * 2), V((chunks, 3, edge, edge), BF16),
+        *([V((groups, 2, edge, fw), BF16)] * 2), V((chunks, 3, edge, edge), BF16),
         *([V((chunks, 2, edge, edge), BF16)] * 2), V((chunks, 3, edge, edge), BF16),
         *([V((chunks, plane, rows_p, edge), link)] * 2),
         V((loops, rows_p, chans), link), V((plane, rows_p, chans), link),
         dma((8,)), dma((groups,)), dma((groups,)), dma((2,)), dma((2,)),
-        *([dma((chunks, 2))] * 8), dma((groups,)), dma((groups,)),
+        *([dma((groups, 2))] * 2), *([dma((chunks, 2))] * 6), dma((groups,)), dma((groups,)),
         *([dma((chunks, plane))] * 2), *([dma((loops,))] * 2), *([dma((plane,))] * 2),
     ]
     out, gf, wf = pl.pallas_call(

time: 46.8 us -> 41.6 us (0.89)
  Pallas kernels: 46 us -> 40.8 us
    pallas_call x1, Pallas kernels: 44.1 us -> 38.9 us  [per_device(): pl.pallas_call(functools.partial(layer_kernel, groups, loops, replicas),...]
where the time goes in v4:
time: 41.6 us; the launch traced here: 41.4 us
  Pallas kernels  40.8 us (98%)
  between operations  0.64 us (2%)
    pallas_call x1, Pallas kernels, per_device(): pl.pallas_call(functools.partial(layer_kernel, groups, loops, replicas),...  38.9 us
    pallas_call x1, Pallas kernels, per_device(): pl.pallas_call(functools.partial(store_kernel, 1.0 / math.sqrt(cells * pl...  1.88 us

profile of v4, /device:TPU:0, one launch (start us, length us, event | category | flops | bytes accessed | tf_op | source)
XLA Modules:
  0.0 41.4 jit_solution(2461374715070706060)
XLA Ops:
  0.6 38.9 %shard_map.94 = (bf16[512,256]{1,0:T(8,128)(2,1)}, bf16[1024,128]{1,0:T(8,128)(2,1)}, bf16[8,32,256]{2,1,0:T(8,128)(2,1)}) custom-call(s32[32]{0:T(128)} %bitcast.11, s32[32]{0:T(128)} %bitcast.12, s32[32]{0:T(128)} %bitcast.13, bf16[1024,128]{1,0:T(8,128)(2,1)} %bitcast.9, bf16[256,256]{1,0:T(8,128)(2,1)} %weight_hbm.1, bf16[32,128,128]{2,1,0:T(8,128)(2,1)} %bitcast.8, ...), custom_call_target="tpu_custom_call" | custom-call | tf_op jit(solution)/shard_map/pallas_call | solution.py:376
  39.6 1.9 %shard_map.95 = (bf16[512,256]{1,0:T(8,128)(2,1)}, bf16[1024,128]{1,0:T(8,128)(2,1)}, f32[256,256]{1,0:T(8,128)}) custom-call(bf16[512,256]{1,0:T(8,128)(2,1)} %get-tuple-element.9.out_in, bf16[1024,128]{1,0:T(8,128)(2,1)} %get-tuple-element.10.gf_in, bf16[8,32,256]{2,1,0:T(8,128)(2,1)} %get-tuple-element.11.wf_in), custom_call_target="tpu_custom_call" | custom-call | tf_op jit(solution)/shard_map/pallas_call | solution.py:390

commit v5 on v4

--- a/solution.py
+++ b/solution.py
@@ -55,6 +55,10 @@
 
     prev_dev = {"loop": loop_peer(loops - 1)}
     next_dev = {"loop": loop_peer(1)}
+    wraps_up = lax.div(my_l + 1, loops)
+    ways = [
+        (d, {"loop": loop_peer((1 - d) * (loops - 1) + d)}) for d in (wraps_up, 1 - wraps_up)
+    ]
 
     def remote(src, dst, ss, rs, dev):
         return pltpu.make_async_remote_copy(
@@ -140,10 +144,9 @@
     def send_sums(sums, send, recv, ss, rs):
         send[0] = sums[0:edge].astype(BF16)
         send[1] = sums[2 * edge:].astype(BF16)
-        pair = (
-            remote(send.at[0], recv.at[1], ss.at[0], rs.at[1], prev_dev),
-            remote(send.at[1], recv.at[0], ss.at[1], rs.at[0], next_dev),
-        )
+        pair = [
+            remote(send.at[d], recv.at[1 - d], ss.at[d], rs.at[1 - d], dev) for d, dev in ways
+        ]
         for copy in pair:
             copy.start()
         return pair
@@ -165,10 +168,9 @@
     y_ref[...] = y32.astype(BF16)
 
     def send_nets(net, ss, rs):
-        pair = (
-            remote(net.at[1], net.at[2], ss.at[0], rs.at[1], prev_dev),
-            remote(net.at[1], net.at[0], ss.at[1], rs.at[0], next_dev),
-        )
+        pair = [
+            remote(net.at[1], net.at[2 - 2 * d], ss.at[d], rs.at[1 - d], dev) for d, dev in ways
+        ]
         for copy in pair:
             copy.start()
         return pair

time: 41.6 us -> 41.1 us (0.988)
  Pallas kernels: 40.8 us -> 40.3 us
    pallas_call x1, Pallas kernels: 38.9 us -> 38.4 us  [per_device(): pl.pallas_call(functools.partial(layer_kernel, groups, loops, replicas),...]
where the time goes in v5:
time: 41.1 us; the launch traced here: 40.9 us
  Pallas kernels  40.3 us (98%)
  between operations  0.64 us (2%)
    pallas_call x1, Pallas kernels, per_device(): pl.pallas_call(functools.partial(layer_kernel, groups, loops, replicas),...  38.4 us
    pallas_call x1, Pallas kernels, per_device(): pl.pallas_call(functools.partial(store_kernel, 1.0 / math.sqrt(cells * pl...  1.88 us

profile of v5, /device:TPU:0, one launch (start us, length us, event | category | flops | bytes accessed | tf_op | source)
XLA Modules:
  0.0 40.9 jit_solution(10805834921296338219)
XLA Ops:
  0.6 38.4 %shard_map.94 = (bf16[512,256]{1,0:T(8,128)(2,1)}, bf16[1024,128]{1,0:T(8,128)(2,1)}, bf16[8,32,256]{2,1,0:T(8,128)(2,1)}) custom-call(s32[32]{0:T(128)} %bitcast.11, s32[32]{0:T(128)} %bitcast.12, s32[32]{0:T(128)} %bitcast.13, bf16[1024,128]{1,0:T(8,128)(2,1)} %bitcast.9, bf16[256,256]{1,0:T(8,128)(2,1)} %weight_hbm.1, bf16[32,128,128]{2,1,0:T(8,128)(2,1)} %bitcast.8, ...), custom_call_target="tpu_custom_call" | custom-call | tf_op jit(solution)/shard_map/pallas_call | solution.py:378
  39.0 1.9 %shard_map.95 = (bf16[512,256]{1,0:T(8,128)(2,1)}, bf16[1024,128]{1,0:T(8,128)(2,1)}, f32[256,256]{1,0:T(8,128)}) custom-call(bf16[512,256]{1,0:T(8,128)(2,1)} %get-tuple-element.9.out_in, bf16[1024,128]{1,0:T(8,128)(2,1)} %get-tuple-element.10.gf_in, bf16[8,32,256]{2,1,0:T(8,128)(2,1)} %get-tuple-element.11.wf_in), custom_call_target="tpu_custom_call" | custom-call | tf_op jit(solution)/shard_map/pallas_call | solution.py:392

commit v6 on v5

--- a/solution.py
+++ b/solution.py
@@ -224,7 +224,7 @@
         q_ref[rows, :] = (dz * root).astype(BF16)
         return carry
 
-    lax.fori_loop(0, cells // step, middle, 0, unroll=2)
+    lax.fori_loop(0, cells // step, middle, 0, unroll=True)
     out_copy = pltpu.make_async_copy(out_ref, out_hbm, local_sem.at[4])
 
     gpart_copies = []

time: 41.1 us -> 40.4 us (0.983)
  Pallas kernels: 40.3 us -> 39.6 us
    pallas_call x1, Pallas kernels: 38.4 us -> 37.8 us  [per_device(): pl.pallas_call(functools.partial(layer_kernel, groups, loops, replicas),...]
where the time goes in v6:
time: 40.4 us; the launch traced here: 40.3 us
  Pallas kernels  39.6 us (98%)
  between operations  0.64 us (2%)
    pallas_call x1, Pallas kernels, per_device(): pl.pallas_call(functools.partial(layer_kernel, groups, loops, replicas),...  37.8 us
    pallas_call x1, Pallas kernels, per_device(): pl.pallas_call(functools.partial(store_kernel, 1.0 / math.sqrt(cells * pl...  1.88 us

profile of v6, /device:TPU:0, one launch (start us, length us, event | category | flops | bytes accessed | tf_op | source)
XLA Modules:
  0.0 40.3 jit_solution(208166150386704690)
XLA Ops:
  0.6 37.8 %shard_map.94 = (bf16[512,256]{1,0:T(8,128)(2,1)}, bf16[1024,128]{1,0:T(8,128)(2,1)}, bf16[8,32,256]{2,1,0:T(8,128)(2,1)}) custom-call(s32[32]{0:T(128)} %bitcast.11, s32[32]{0:T(128)} %bitcast.12, s32[32]{0:T(128)} %bitcast.13, bf16[1024,128]{1,0:T(8,128)(2,1)} %bitcast.9, bf16[256,256]{1,0:T(8,128)(2,1)} %weight_hbm.1, bf16[32,128,128]{2,1,0:T(8,128)(2,1)} %bitcast.8, ...), custom_call_target="tpu_custom_call" | custom-call | tf_op jit(solution)/shard_map/pallas_call | solution.py:378
  38.4 1.9 %shard_map.95 = (bf16[512,256]{1,0:T(8,128)(2,1)}, bf16[1024,128]{1,0:T(8,128)(2,1)}, f32[256,256]{1,0:T(8,128)}) custom-call(bf16[512,256]{1,0:T(8,128)(2,1)} %get-tuple-element.9.out_in, bf16[1024,128]{1,0:T(8,128)(2,1)} %get-tuple-element.10.gf_in, bf16[8,32,256]{2,1,0:T(8,128)(2,1)} %get-tuple-element.11.wf_in), custom_call_target="tpu_custom_call" | custom-call | tf_op jit(solution)/shard_map/pallas_call | solution.py:392
